TPU v7x, 32 devices: a whole 2x2x4 slice. The times are simulated.
32 devices in a mesh: dp: 32 (over z, y, x, core).
Axes of the slice: x: 2, y: 2, z: 4, core: 2. Of those that a mesh axis runs over, the one named last changes fastest.
Arguments:
- tokens: bfloat16 [2, 4096, 896], P(None, 'dp'), may hold values from -6 to 6
- positions: int32 [2, 4096], P(None, 'dp'), may hold values from 0 to 127, as said below
- cotangent: bfloat16 [2, 4096, 896], P(None, 'dp'), may hold values from -6 to 6
- norm_attn: bfloat16 [896], P('dp'), may hold values from 0.099609375 to 1.8984375
- w_query: bfloat16 [802816], P('dp'), may hold values from -0.1875 to 0.1875
- b_query: bfloat16 [896], P('dp'), may hold values from -3 to 3
- w_key: bfloat16 [114688], P('dp'), may hold values from -0.1875 to 0.1875
- b_key: bfloat16 [128], replicated, may hold values from -3 to 3
- w_value: bfloat16 [114688], P('dp'), may hold values from -0.1875 to 0.1875
- b_value: bfloat16 [128], P('dp'), may hold values from -3 to 3
- w_out: bfloat16 [802816], P('dp'), may hold values from -1.5 to 1.5
- norm_ffn: bfloat16 [896], P('dp'), may hold values from 0.099609375 to 1.8984375
- w_gate: bfloat16 [4358144], P('dp'), may hold values from -0.1875 to 0.1875
- w_up: bfloat16 [4358144], P('dp'), may hold values from -0.1875 to 0.1875
- w_down: bfloat16 [4358144], P('dp'), may hold values from -0.078125 to 0.078125
Outputs:
- block_out: bfloat16 [2, 4096, 896], P(None, 'dp')
- grad_input: bfloat16 [2, 4096, 896], P(None, 'dp')
- grad_norm_attn: float32 [896], P('dp')
- grad_query: float32 [802816], P('dp')
- grad_bquery: float32 [896], P('dp')
- grad_key: float32 [114688], P('dp')
- grad_bkey: float32 [128], replicated
- grad_value: float32 [114688], P('dp')
- grad_bvalue: float32 [128], P('dp')
- grad_out: float32 [802816], P('dp')
- grad_norm_ffn: float32 [896], P('dp')
- grad_gate: float32 [4358144], P('dp')
- grad_up: float32 [4358144], P('dp')
- grad_down: float32 [4358144], P('dp')
Inputs may be any that keep to these rules, and one draw needn't show every extreme that they name: `positions`: within each block of 128 tokens of one micro-batch the first position is 0; from token to token a position either rises by one (same sequence) or is 0 (a new sequence begins).
All inputs are finite; a program needn't handle non-finite values.
Results may differ from a plain program's by a relative error of at most 0.023.
Values may be sent and summed in bfloat16 or wider, within the bound.
A program may use at most 256 MiB of HBM per device.

v0:
```python
import jax
import jax.numpy as jnp
from jax import lax
from jax.sharding import PartitionSpec as P

HEADS = 14
KV_HEADS = 2
HEAD_DIM = 64


def rms_scale(field):
    return lax.rsqrt(jnp.mean(field * field, axis=-1, keepdims=True) + 1e-06)


def product(left, right):
    return jnp.dot(left, right, preferred_element_type=jnp.float32)


def rope_tables(positions):
    half_dim = HEAD_DIM // 2
    inv_freq = 1000000.0 ** (-(jnp.arange(half_dim).astype(jnp.float32) * 2.0 / HEAD_DIM))
    angles = positions.astype(jnp.float32)[:, None] * inv_freq[None, :]
    angles = jnp.concatenate([angles, angles], axis=-1)
    return (jnp.cos(angles)[:, None, :], jnp.sin(angles)[:, None, :])


def rotate(field, cosine, sine_table):
    half_dim = HEAD_DIM // 2
    turned = jnp.concatenate([-field[..., half_dim:], field[..., :half_dim]], axis=-1)
    return field * cosine + turned * sine_table


def rotate_back(field, cosine, sine_table):
    half_dim = HEAD_DIM // 2
    moved = field * sine_table
    return field * cosine + jnp.concatenate(
        [moved[..., half_dim:], -moved[..., :half_dim]], axis=-1
    )


def norm_back(grad_normed, field, scale, gain):
    weighted = grad_normed * gain
    grad_gain = jnp.sum(grad_normed * field * scale, axis=0)
    grad_field = weighted * scale - field * (scale * scale * scale) * jnp.mean(
        weighted * field, axis=-1, keepdims=True
    )
    return (grad_gain, grad_field)


def attention_mask(positions):
    slots = positions.shape[0]
    row_index = jnp.arange(slots, dtype=jnp.int32)
    seq_start = row_index - positions
    return (seq_start[:, None] == seq_start[None, :]) & (row_index[:, None] >= row_index[None, :])


def score_table(query, key_rot, allowed):
    scores = (
        jnp.einsum("qhgd,khd->hgqk", query, key_rot, preferred_element_type=jnp.float32) * 0.125
    )
    return jnp.where(allowed[None, None], scores, -1e30)


def matrix_views(gathered, b_key):
    norm_attn, w_query, b_query, w_key, w_value, b_value, w_out, norm_ffn, w_gate, w_up, w_down = (
        gathered
    )
    width = norm_attn.shape[0]
    return (
        norm_attn,
        w_query.reshape(width, -1),
        b_query,
        w_key.reshape(width, -1),
        b_key,
        w_value.reshape(width, -1),
        b_value,
        w_out.reshape(-1, width),
        norm_ffn,
        w_gate.reshape(width, -1),
        w_up.reshape(width, -1),
        w_down.reshape(-1, width),
    )


def spread_small(grad_list, copies):
    return grad_list[:4] + (jnp.tile(grad_list[4][None, :], (copies, 1)),) + grad_list[5:]


def gather_small(summed):
    return summed[:4] + (summed[4].reshape(-1),) + summed[5:]


def forward_pass(params, block_in, positions):
    (
        norm_attn,
        w_query,
        b_query,
        w_key,
        b_key,
        w_value,
        b_value,
        w_out,
        norm_ffn,
        w_gate,
        w_up,
        w_down,
    ) = params
    slots = block_in.shape[0]
    group_size = HEADS // KV_HEADS
    inputs = block_in.astype(jnp.float32)
    scale_attn = rms_scale(inputs)
    normed = (inputs * scale_attn * norm_attn.astype(jnp.float32)).astype(jnp.bfloat16)
    query_lin = product(normed, w_query) + b_query.astype(jnp.float32)
    key_lin = product(normed, w_key) + b_key.astype(jnp.float32)
    value_lin = product(normed, w_value) + b_value.astype(jnp.float32)
    cosine, sine_table = rope_tables(positions)
    query = rotate(query_lin.reshape(slots, HEADS, HEAD_DIM), cosine, sine_table).astype(
        jnp.bfloat16
    )
    query = query.reshape(slots, KV_HEADS, group_size, HEAD_DIM)
    key_rot = rotate(key_lin.reshape(slots, KV_HEADS, HEAD_DIM), cosine, sine_table).astype(
        jnp.bfloat16
    )
    values = value_lin.reshape(slots, KV_HEADS, HEAD_DIM).astype(jnp.bfloat16)
    allowed = attention_mask(positions)
    scores = score_table(query, key_rot, allowed)
    row_max = jnp.max(scores, axis=-1, keepdims=True)
    expo = jnp.exp(scores - row_max)
    row_sum = jnp.sum(expo, axis=-1, keepdims=True)
    attn_probs = (expo / row_sum).astype(jnp.bfloat16)
    mixed_heads = jnp.einsum(
        "hgqk,khd->qhgd", attn_probs, values, preferred_element_type=jnp.float32
    )
    mixed_heads = mixed_heads.reshape(slots, HEADS * HEAD_DIM).astype(jnp.bfloat16)
    hidden = inputs + product(mixed_heads, w_out)
    scale_ffn = rms_scale(hidden)
    normed_ffn = (hidden * scale_ffn * norm_ffn.astype(jnp.float32)).astype(jnp.bfloat16)
    gate_pre = product(normed_ffn, w_gate)
    up_pre = product(normed_ffn, w_up)
    hidden_act = (jax.nn.silu(gate_pre) * up_pre).astype(jnp.bfloat16)
    block_out = (hidden + product(hidden_act, w_down)).astype(jnp.bfloat16)
    kept = (
        inputs,
        scale_attn,
        normed,
        query,
        key_rot,
        values,
        allowed,
        row_max,
        row_sum,
        mixed_heads,
        hidden,
        scale_ffn,
        normed_ffn,
        gate_pre,
        up_pre,
        hidden_act,
        cosine,
        sine_table,
    )
    return (block_out, kept)


def backward_pass(params, kept, block_grad):
    (
        norm_attn,
        w_query,
        b_query,
        w_key,
        b_key,
        w_value,
        b_value,
        w_out,
        norm_ffn,
        w_gate,
        w_up,
        w_down,
    ) = params
    (
        inputs,
        scale_attn,
        normed,
        query,
        key_rot,
        values,
        allowed,
        row_max,
        row_sum,
        mixed_heads,
        hidden,
        scale_ffn,
        normed_ffn,
        gate_pre,
        up_pre,
        hidden_act,
        cosine,
        sine_table,
    ) = kept
    slots = block_grad.shape[0]
    group_size = HEADS // KV_HEADS
    grad_top = block_grad.astype(jnp.float32)
    grad_down = jnp.einsum("sf,sd->fd", hidden_act, block_grad, preferred_element_type=jnp.float32)
    grad_act = jnp.einsum("sd,fd->sf", block_grad, w_down, preferred_element_type=jnp.float32)
    sigma = jax.nn.sigmoid(gate_pre)
    grad_gate_pre = (grad_act * up_pre * (sigma + gate_pre * sigma * (1.0 - sigma))).astype(
        jnp.bfloat16
    )
    grad_up_pre = (grad_act * (gate_pre * sigma)).astype(jnp.bfloat16)
    grad_gate = jnp.einsum(
        "sc,sf->cf", normed_ffn, grad_gate_pre, preferred_element_type=jnp.float32
    )
    grad_up = jnp.einsum("sc,sf->cf", normed_ffn, grad_up_pre, preferred_element_type=jnp.float32)
    grad_normed_ffn = jnp.einsum(
        "sf,cf->sc", grad_gate_pre, w_gate, preferred_element_type=jnp.float32
    )
    grad_normed_ffn = grad_normed_ffn + jnp.einsum(
        "sf,cf->sc", grad_up_pre, w_up, preferred_element_type=jnp.float32
    )
    grad_norm_ffn, grad_hidden_part = norm_back(
        grad_normed_ffn, hidden, scale_ffn, norm_ffn.astype(jnp.float32)
    )
    grad_hidden = grad_top + grad_hidden_part
    grad_attn = grad_hidden.astype(jnp.bfloat16)
    grad_wout = jnp.einsum("se,sd->ed", mixed_heads, grad_attn, preferred_element_type=jnp.float32)
    grad_mixed = jnp.einsum("sd,ed->se", grad_attn, w_out, preferred_element_type=jnp.float32)
    grad_mixed = grad_mixed.astype(jnp.bfloat16).reshape(slots, KV_HEADS, group_size, HEAD_DIM)
    scores = score_table(query, key_rot, allowed)
    attn_probs = jnp.exp(scores - row_max) / row_sum
    probs_low = attn_probs.astype(jnp.bfloat16)
    grad_values = jnp.einsum(
        "hgqk,qhgd->khd", probs_low, grad_mixed, preferred_element_type=jnp.float32
    )
    grad_probs = jnp.einsum(
        "qhgd,khd->hgqk", grad_mixed, values, preferred_element_type=jnp.float32
    )
    row_delta = jnp.sum(grad_probs * attn_probs, axis=-1, keepdims=True)
    grad_scores = (attn_probs * (grad_probs - row_delta)).astype(jnp.bfloat16)
    grad_query_rot = 0.125 * jnp.einsum(
        "hgqk,khd->qhgd", grad_scores, key_rot, preferred_element_type=jnp.float32
    )
    grad_key_rot = 0.125 * jnp.einsum(
        "hgqk,qhgd->khd", grad_scores, query, preferred_element_type=jnp.float32
    )
    grad_qlin = rotate_back(grad_query_rot.reshape(slots, HEADS, HEAD_DIM), cosine, sine_table)
    grad_qlin = grad_qlin.reshape(slots, HEADS * HEAD_DIM).astype(jnp.bfloat16)
    grad_klin = (
        rotate_back(grad_key_rot, cosine, sine_table)
        .reshape(slots, KV_HEADS * HEAD_DIM)
        .astype(jnp.bfloat16)
    )
    grad_vlin = grad_values.reshape(slots, KV_HEADS * HEAD_DIM).astype(jnp.bfloat16)
    grad_wquery = jnp.einsum("sc,se->ce", normed, grad_qlin, preferred_element_type=jnp.float32)
    grad_wkey = jnp.einsum("sc,se->ce", normed, grad_klin, preferred_element_type=jnp.float32)
    grad_wvalue = jnp.einsum("sc,se->ce", normed, grad_vlin, preferred_element_type=jnp.float32)
    grad_bquery = jnp.sum(grad_qlin.astype(jnp.float32), axis=0)
    grad_bkey = jnp.sum(grad_klin.astype(jnp.float32), axis=0)
    grad_bvalue = jnp.sum(grad_vlin.astype(jnp.float32), axis=0)
    grad_normed = jnp.einsum("se,ce->sc", grad_qlin, w_query, preferred_element_type=jnp.float32)
    grad_normed = grad_normed + jnp.einsum(
        "se,ce->sc", grad_klin, w_key, preferred_element_type=jnp.float32
    )
    grad_normed = grad_normed + jnp.einsum(
        "se,ce->sc", grad_vlin, w_value, preferred_element_type=jnp.float32
    )
    grad_norm_attn, grad_input_part = norm_back(
        grad_normed, inputs, scale_attn, norm_attn.astype(jnp.float32)
    )
    grad_input = (grad_hidden + grad_input_part).astype(jnp.bfloat16)
    grad_list = (
        grad_norm_attn,
        grad_wquery.reshape(-1),
        grad_bquery,
        grad_wkey.reshape(-1),
        grad_bkey,
        grad_wvalue.reshape(-1),
        grad_bvalue,
        grad_wout.reshape(-1),
        grad_norm_ffn,
        grad_gate.reshape(-1),
        grad_up.reshape(-1),
        grad_down.reshape(-1),
    )
    return (grad_list, grad_input)


def per_device(
    tokens,
    positions,
    cotangent,
    norm_attn,
    w_query,
    b_query,
    w_key,
    b_key,
    w_value,
    b_value,
    w_out,
    norm_ffn,
    w_gate,
    w_up,
    w_down,
):
    copies = lax.axis_size("dp")
    totals = None
    outputs = []
    input_grads = []
    for micro_step in range(tokens.shape[0]):
        params = matrix_views(
            (
                lax.all_gather(norm_attn, "dp", axis=0, tiled=True),
                lax.all_gather(w_query, "dp", axis=0, tiled=True),
                lax.all_gather(b_query, "dp", axis=0, tiled=True),
                lax.all_gather(w_key, "dp", axis=0, tiled=True),
                lax.all_gather(w_value, "dp", axis=0, tiled=True),
                lax.all_gather(b_value, "dp", axis=0, tiled=True),
                lax.all_gather(w_out, "dp", axis=0, tiled=True),
                lax.all_gather(norm_ffn, "dp", axis=0, tiled=True),
                lax.all_gather(w_gate, "dp", axis=0, tiled=True),
                lax.all_gather(w_up, "dp", axis=0, tiled=True),
                lax.all_gather(w_down, "dp", axis=0, tiled=True),
            ),
            b_key,
        )
        block_out, kept = forward_pass(params, tokens[micro_step], positions[micro_step])
        outputs.append(block_out)
        params = matrix_views(
            (
                lax.all_gather(norm_attn, "dp", axis=0, tiled=True),
                lax.all_gather(w_query, "dp", axis=0, tiled=True),
                lax.all_gather(b_query, "dp", axis=0, tiled=True),
                lax.all_gather(w_key, "dp", axis=0, tiled=True),
                lax.all_gather(w_value, "dp", axis=0, tiled=True),
                lax.all_gather(b_value, "dp", axis=0, tiled=True),
                lax.all_gather(w_out, "dp", axis=0, tiled=True),
                lax.all_gather(norm_ffn, "dp", axis=0, tiled=True),
                lax.all_gather(w_gate, "dp", axis=0, tiled=True),
                lax.all_gather(w_up, "dp", axis=0, tiled=True),
                lax.all_gather(w_down, "dp", axis=0, tiled=True),
            ),
            b_key,
        )
        grad_list, grad_input = backward_pass(params, kept, cotangent[micro_step])
        input_grads.append(grad_input)
        totals = grad_list if micro_step == 0 else jax.tree.map(jnp.add, totals, grad_list)
    sectioned = spread_small(totals, copies)
    summed = gather_small(
        (
            lax.psum_scatter(sectioned[0], "dp", scatter_dimension=0, tiled=True),
            lax.psum_scatter(sectioned[1], "dp", scatter_dimension=0, tiled=True),
            lax.psum_scatter(sectioned[2], "dp", scatter_dimension=0, tiled=True),
            lax.psum_scatter(sectioned[3], "dp", scatter_dimension=0, tiled=True),
            lax.psum_scatter(sectioned[4], "dp", scatter_dimension=0, tiled=True),
            lax.psum_scatter(sectioned[5], "dp", scatter_dimension=0, tiled=True),
            lax.psum_scatter(sectioned[6], "dp", scatter_dimension=0, tiled=True),
            lax.psum_scatter(sectioned[7], "dp", scatter_dimension=0, tiled=True),
            lax.psum_scatter(sectioned[8], "dp", scatter_dimension=0, tiled=True),
            lax.psum_scatter(sectioned[9], "dp", scatter_dimension=0, tiled=True),
            lax.psum_scatter(sectioned[10], "dp", scatter_dimension=0, tiled=True),
            lax.psum_scatter(sectioned[11], "dp", scatter_dimension=0, tiled=True),
        )
    )
    return (
        jnp.stack(outputs),
        jnp.stack(input_grads),
        summed[0],
        summed[1],
        summed[2],
        summed[3],
        summed[4],
        summed[5],
        summed[6],
        summed[7],
        summed[8],
        summed[9],
        summed[10],
        summed[11],
    )


def solution(mesh):
    in_specs = (
        P(None, "dp", None),
        P(None, "dp"),
        P(None, "dp", None),
        P("dp"),
        P("dp"),
        P("dp"),
        P("dp"),
        P(),
        P("dp"),
        P("dp"),
        P("dp"),
        P("dp"),
        P("dp"),
        P("dp"),
        P("dp"),
    )
    out_specs = (
        P(None, "dp", None),
        P(None, "dp", None),
        P("dp"),
        P("dp"),
        P("dp"),
        P("dp"),
        P(),
        P("dp"),
        P("dp"),
        P("dp"),
        P("dp"),
        P("dp"),
        P("dp"),
        P("dp"),
    )
    return jax.shard_map(
        per_device, mesh=mesh, in_specs=in_specs, out_specs=out_specs, check_vma=False
    )
```

profile of v0, /device:TPU:0, one launch (start us, length us, event | category | flops | bytes accessed | tf_op | source)
XLA Modules:
  0.0 1446.4 jit_solution(3403692117063924073)
XLA Ops:
  16.4 42.3 %all-reduce.18 = (bf16[128]{0:T(256)(128)(2,1)S(1)}, bf16[896]{0:T(1024)(128)(2,1)S(1)}, bf16[896]{0:T(1024)(128)(2,1)S(1)}, bf16[896]{0:T(1024)(128)(2,1)S(1)}) all-reduce(bf16[128]{0:T(256)(128)(2,1)S(1)} %dynamic-update-slice.1, bf16[896]{0:T(1024)(128)(2,1)S(1)} %dynamic-update-slice, ...), channel_id=1, replica_groups=mesh['dp'=32] {'dp'}, use_global_device_ids=true, to_apply=%add.1 | all-reduce | flops 2816 | bytes 11264
  60.2 41.5 %all-gather = bf16[32,1,3584]{2,1,0:T(2,128)(2,1)S(1)} all-gather(bf16[1,1,3584]{2,1,0:T(2,128)(2,1)S(1)} %reshape.732), channel_id=1, replica_groups=mesh['dp'=32] {'dp'}, dimensions={0}, use_global_device_ids=true | all-gather | bytes 236544 | tf_op jit(solution)/shard_map/all_gather | solution.py:315
  103.4 38.4 %all-gather.1 = bf16[32,1,3584]{2,1,0:T(2,128)(2,1)S(1)} all-gather(bf16[1,1,3584]{2,1,0:T(2,128)(2,1)S(1)} %reshape.734), channel_id=1, replica_groups=mesh['dp'=32] {'dp'}, dimensions={0}, use_global_device_ids=true | all-gather | bytes 236544 | tf_op jit(solution)/shard_map/all_gather | solution.py:314
  148.4 11.0 reduce.10
  161.9 12.4 reduce.11
  196.6 19.3 %all-gather.10.cloned.1.call-done = bf16[4358144]{0:T(1024)(128)(2,1)} async-done(((bf16[136192]{0:T(1024)(128)(2,1)}), bf16[4358144]{0:T(1024)(128)(2,1)}) %all-gather.10.cloned.1.call-update) | async-done | bytes 8716304 | tf_op jit(solution)/shard_map/all_gather | solution.py:319
  216.0 16.4 %reshape.711 = bf16[896,4864]{1,0:T(8,128)(2,1)} reshape(bf16[4358144]{0:T(1024)(128)(2,1)} %all-gather.10.cloned.1.call-done) | data formatting | bytes 17432576 | tf_op jit(solution)/shard_map/reshape | solution.py:79
  232.4 63.4 %all-gather.12.cloned.1.call-done = bf16[4358144]{0:T(1024)(128)(2,1)} async-done(((bf16[136192]{0:T(1024)(128)(2,1)}), bf16[4358144]{0:T(1024)(128)(2,1)}) %all-gather.12.cloned.1.call-update) | async-done | bytes 8716304 | tf_op jit(solution)/shard_map/all_gather | solution.py:320
  295.8 16.4 %reshape.712 = bf16[896,4864]{1,0:T(8,128)(2,1)} reshape(bf16[4358144]{0:T(1024)(128)(2,1)} %all-gather.12.cloned.1.call-done) | data formatting | bytes 17432576 | tf_op jit(solution)/shard_map/reshape | solution.py:80
  321.7 53.9 %all-gather.14.cloned.1.call-done = bf16[4358144]{0:T(1024)(128)(2,1)} async-done(((bf16[136192]{0:T(1024)(128)(2,1)}), bf16[4358144]{0:T(1024)(128)(2,1)}) %all-gather.14.cloned.1.call-update) | async-done | bytes 8716304 | tf_op jit(solution)/shard_map/all_gather | solution.py:321
  375.6 16.6 %reshape.713 = bf16[4864,896]{1,0:T(8,128)(2,1)} reshape(bf16[4358144]{0:T(1024)(128)(2,1)} %all-gather.14.cloned.1.call-done) | data formatting | bytes 17432576 | tf_op jit(solution)/shard_map/reshape | solution.py:81
  392.2 9.0 multiply_convert_fusion.2
  401.2 6.8 fusion.129
  418.4 9.4 multiply_convert_fusion
  438.4 8.4 fusion.134
  446.9 8.5 fusion.133
  484.5 14.4 convolution_add_fusion.1
  498.9 17.9 %add.355 = f32[4358144]{0:T(1024)} reshape(f32[896,4864]{1,0:T(8,128)} %convolution_add_fusion.1) | data formatting | bytes 34865152 | tf_op jit(solution)/shard_map/add | solution.py:345
  516.8 14.5 %convolution_add_fusion.2 = f32[896,4864]{1,0:T(8,128)} fusion(f32[896,4864]{1,0:T(8,128)} %fusion.133, bf16[128,896]{1,0:T(8,128)(2,1)S(1)} %get-tuple-element.80, bf16[128,4864]{1,0:T(8,128)(2,1)S(1)} %copy-done.25), kind=kOutput, calls=%fused_computation.4 | convolution fusion | flops 1120043008 | bytes 36339712 | tf_op jit(solution)/shard_map/sc,sf->cf/dot_general | solution.py:210
  531.2 17.8 %add.353 = f32[4358144]{0:T(1024)} reshape(f32[896,4864]{1,0:T(8,128)} %convolution_add_fusion.2) | data formatting | bytes 34865152 | tf_op jit(solution)/shard_map/add | solution.py:345
  552.8 9.8 convolution_add_fusion
  562.5 18.7 %add.357 = f32[4358144]{0:T(1024)} reshape(f32[4864,896]{1,0:T(8,128)} %convolution_add_fusion) | data formatting | bytes 34865152 | tf_op jit(solution)/shard_map/add | solution.py:345
  596.5 41.6 %all-reduce.16 = (f32[896]{0:T(1024)S(1)}, f32[896]{0:T(1024)S(1)}, f32[32,128]{1,0:T(8,128)S(1)}, f32[128]{0:T(128)S(1)}, f32[896]{0:T(1024)S(1)}) all-reduce(f32[896]{0:T(1024)S(1)} %add.334, f32[896]{0:T(1024)S(1)} %add.340, f32[32,128]{1,0:T(8,128)S(1)} %tile.2, f32[128]{0:T(128)S(1)} %copy-done.97, ...), channel_id=2, replica_groups=mesh['dp'=32] {'dp'}, use_global_device_ids=true, to_apply=%region_16.17.clone | all-reduce | flops 6912 | bytes 55296
  651.7 776.0 %all-reduce.21.cloned.1.call-done = (f32[802816]{0:T(1024)}, f32[114688]{0:T(1024)}, f32[114688]{0:T(1024)}, f32[802816]{0:T(1024)}, f32[4358144]{0:T(1024)}, /*index=5*/f32[4358144]{0:T(1024)}, f32[4358144]{0:T(1024)}) async-done(((f32[802816]{0:T(1024)}, f32[114688]{0:T(1024)}, f32[114688]{0:T(1024)}, f32[802816]{0:T(1024)}, f32[4358144]{0:T(1024)}, /*index=5*/f32[4358144]{0:T(1024)}, f32[4358144]{0:T(1024)}), ...) | async-done | bytes 59637776
  (378 shorter events, 146.2 us)
Async XLA Ops:
  7.2 136.3 %copy-start.94 = (s32[2,128]{1,0:T(2,128)S(1)}, s32[2,128]{1,0:T(2,128)}, u32[]{:S(2)}) copy-start(s32[2,128]{1,0:T(2,128)} %param.16) | copy-start | bytes 3076
  7.2 137.2 %copy-start.3 = (bf16[2,128,896]{2,1,0:T(8,128)(2,1)S(1)}, bf16[2,128,896]{2,1,0:T(8,128)(2,1)}, u32[]{:S(2)}) copy-start(bf16[2,128,896]{2,1,0:T(8,128)(2,1)} %param.15) | copy-start | bytes 1376260
  7.2 141.2 %all-gather.16.cloned.1.call-start = ((), (), s32[]{:S(2)}) async-start(), calls=%async_computation.3 | async-start | bytes 3311616 | tf_op jit(solution)/shard_map/all_gather | solution.py:312
  8.8 153.1 %all-gather.18.cloned.1.call-start = ((), (), s32[]{:S(2)}) async-start(), calls=%async_computation.4 | async-start | bytes 3311616 | tf_op jit(solution)/shard_map/all_gather | solution.py:317
  10.4 205.6 %all-gather.10.cloned.1.call-start = ((), (), s32[]{:S(2)}) async-start(), calls=%async_computation | async-start | bytes 8988672 | tf_op jit(solution)/shard_map/all_gather | solution.py:319
  11.1 284.7 %all-gather.12.cloned.1.call-start = ((), (), s32[]{:S(2)}) async-start(), calls=%async_computation.1 | async-start | bytes 8988672 | tf_op jit(solution)/shard_map/all_gather | solution.py:320
  11.7 363.9 %all-gather.14.cloned.1.call-start = ((), (), s32[]{:S(2)}) async-start(), calls=%async_computation.2 | async-start | bytes 8988672 | tf_op jit(solution)/shard_map/all_gather | solution.py:321
  12.3 1415.4 %all-reduce.21.cloned.1.call-start = ((), (), s32[]{:S(2)}) async-start(), calls=%async_computation.5 | async-start | bytes 119275520
  103.4 44.1 %copy-start.51 = (bf16[896,128]{1,0:T(8,128)(2,1)}, bf16[896,128]{1,0:T(8,128)(2,1)S(1)}, u32[]{:S(2)}) copy-start(bf16[896,128]{1,0:T(8,128)(2,1)S(1)} %reshape.704) | copy-start | bytes 688132
  144.3 42.8 %copy-start.62 = (f32[128,64]{0,1:T(8,128)}, f32[128,64]{0,1:T(8,128)S(1)}, u32[]{:S(2)}) copy-start(f32[128,64]{0,1:T(8,128)S(1)} %get-tuple-element.78) | copy-start | bytes 98308
  147.1 42.7 %copy-start.76 = (bf16[128,2,64,1]{0,2,3,1:T(8,128)(2,1)}, bf16[128,2,64,1]{0,2,3,1:T(8,128)(2,1)S(1)}, u32[]{:S(2)}) copy-start(bf16[128,2,64,1]{0,2,3,1:T(8,128)(2,1)S(1)} %fusion.90) | copy-start | bytes 98308
  147.4 42.3 %copy-start.101 = (bf16[128,128]{0,1:T(8,128)(2,1)}, bf16[128,128]{0,1:T(8,128)(2,1)S(1)}, u32[]{:S(2)}) copy-start(bf16[128,128]{0,1:T(8,128)(2,1)S(1)} %fusion.21) | copy-start | bytes 98308
  161.9 20.6 %copy-start.1 = (bf16[896,896]{1,0:T(8,128)(2,1)}, bf16[896,896]{1,0:T(8,128)(2,1)S(1)}, u32[]{:S(2)}) copy-start(bf16[896,896]{1,0:T(8,128)(2,1)S(1)} %reshape.707) | copy-start | bytes 4816900
  192.2 215.9 %copy-start.92 = (f32[128]{0:T(128)}, f32[128]{0:T(128)S(1)}, u32[]{:S(2)}) copy-start(f32[128]{0:T(128)S(1)} %get-tuple-element.94) | copy-start | bytes 1540
  194.5 261.9 %copy-start.88 = (f32[2,7,128]{2,1,0:T(8,128)}, f32[2,7,128]{2,1,0:T(8,128)S(1)}, u32[]{:S(2)}) copy-start(f32[2,7,128]{2,1,0:T(8,128)S(1)} %get-tuple-element.99) | copy-start | bytes 21508
  195.9 36.5 %copy-start.60 = (bf16[2,64,7,128]{3,1,2,0:T(8,128)(2,1)}, bf16[2,64,7,128]{3,1,2,0:T(8,128)(2,1)S(1)}, u32[]{:S(2)}) copy-start(bf16[2,64,7,128]{3,1,2,0:T(8,128)(2,1)S(1)} %convolution_convert_fusion.3) | copy-start | bytes 688132
  196.5 35.9 %copy-start.8 = (f32[128,896]{1,0:T(8,128)}, f32[128,896]{1,0:T(8,128)S(1)}, u32[]{:S(2)}) copy-start(f32[128,896]{1,0:T(8,128)S(1)} %get-tuple-element.102) | copy-start | bytes 1376260
  196.6 122.2 %copy-start.15 = (bf16[128,896]{1,0:T(8,128)(2,1)}, bf16[128,896]{1,0:T(8,128)(2,1)S(1)}, u32[]{:S(2)}) copy-start(bf16[128,896]{1,0:T(8,128)(2,1)S(1)} %multiply_convert_fusion.9) | copy-start | bytes 688132
  375.6 32.4 %slice-start.3 = ((s8[8716288]{0:T(1024)(128)(4,1)}), s8[327680]{0:T(1024)(128)(4,1)S(1)}, s32[]{:S(2)}) async-start(s8[8716288]{0:T(1024)(128)(4,1)} %bitcast.340), calls=%async_computation.9 | async-start | bytes 655360
  435.5 33.4 %copy-start.17 = (f32[128,896]{1,0:T(8,128)}, f32[128,896]{1,0:T(8,128)S(1)}, u32[]{:S(2)}) copy-start(f32[128,896]{1,0:T(8,128)S(1)} %get-tuple-element.55) | copy-start | bytes 1376260
  562.5 19.9 %copy-start.78 = (f32[128,2,32]{0,2,1:T(8,128)S(1)}, f32[128,2,32]{0,2,1:T(8,128)}, u32[]{:S(2)}) copy-start(f32[128,2,32]{0,2,1:T(8,128)} %get-tuple-element.66) | copy-start | bytes 98308
  562.5 20.6 %copy-start.43 = (f32[896,128]{1,0:T(8,128)S(1)}, f32[896,128]{1,0:T(8,128)}, u32[]{:S(2)}) copy-start(f32[896,128]{1,0:T(8,128)} %fusion.104) | copy-start | bytes 1376260
  595.1 45.9 %copy-start.11 = (f32[128,896]{1,0:T(8,128)S(1)}, f32[128,896]{1,0:T(8,128)}, u32[]{:S(2)}) copy-start(f32[128,896]{1,0:T(8,128)} %copy-done.8) | copy-start | bytes 1376260
  595.1 51.6 %slice-start.6 = ((s8[8716288]{0:T(1024)(128)(4,1)}), s8[327680]{0:T(1024)(128)(4,1)S(1)}, s32[]{:S(2)}) async-start(s8[8716288]{0:T(1024)(128)(4,1)} %bitcast.342), calls=%async_computation.12 | async-start | bytes 655360
  (94 other events, 500.1 us)
Sparse Core Ops, SparseCore 0:
  11.5 61.7 all-gather.15
  76.8 59.0 all-gather.17
  138.8 77.1 all-gather.9
  218.7 77.0 all-gather.11
  298.5 76.9 all-gather.13
  584.4 843.2 all-reduce.20
where the time goes:
time: 1450 us
  waiting for transfers between devices  914 us (63%)
  blocking collectives  164 us (11%)
  matrix products  157 us (11%)
  local copies, waits for them, and re-layouts  152 us (10%)
  other arithmetic  43.2 us (3%)
  between operations  15.9 us (1%)
    unnamed x7, waiting for transfers between devices  778 us
    unnamed x2, blocking collectives  83.9 us
    add x8, local copies, waits for them, and re-layouts, per_device(): jax.tree.map(jnp.add, totals, grad_list)  66.4 us
    all_gather x1, waiting for transfers between devices, per_device(): lax.all_gather(w_up, 'dp', axis=0, tiled=True)  63.4 us
    all_gather x1, waiting for transfers between devices, per_device(): lax.all_gather(w_down, 'dp', axis=0, tiled=True)  53.9 us
    all_gather x1, blocking collectives, per_device(): lax.all_gather(w_value, 'dp', axis=0, tiled=True)  41.5 us
    all_gather x1, blocking collectives, per_device(): lax.all_gather(w_key, 'dp', axis=0, tiled=True)  38.4 us
    dot_general x14, matrix products, product(): return jnp.dot(left, right, preferred_element_type=jnp.float32)  30.8 us
  transfers between devices with their start and end apart: 6, of which 4 were waited for; matrix products, arithmetic and copies ran while one was open for 9% of the time, Pallas kernels for 0%

commit v1 on v0

v1 whole, which is shorter than its diff:
```python
import functools

import jax
import jax.numpy as jnp
from jax import lax
from jax.experimental import pallas as pl
from jax.experimental.pallas import tpu as pltpu
from jax.sharding import PartitionSpec as P

HEADS = 14
KV_HEADS = 2
HEAD_DIM = 64
GROUP = HEADS // KV_HEADS
PLANE = 8
CHIPS = 4
LANES = 128
FIELD = 32
MESH = pl.DeviceIdType.MESH
F32 = jnp.float32
BF16 = jnp.bfloat16


def up(value, step):
    return -(-value // step) * step


def mm(left, right, dims=((1,), (0,))):
    return lax.dot_general(left, right, (dims, ((), ())), preferred_element_type=F32)


def mm_nt(left, right):
    return mm(left, right, ((1,), (1,)))


def mm_tn(left, right):
    return mm(left, right, ((0,), (0,)))


def split_mm(left, right, nt=False):
    high = left.astype(BF16)
    low = (left - high.astype(F32)).astype(BF16)
    dot = mm_nt if nt else mm
    return dot(high, right) + dot(low, right)


def iota(shape, dim):
    return lax.broadcasted_iota(jnp.int32, shape, dim)


class Dims:
    def __init__(self, n, d, ff, slots, micro):
        self.n, self.d, self.ff = n, d, ff
        self.planes = n // PLANE
        self.rows = d // n
        self.rp = 8
        while self.rp < self.rows + 1:
            self.rp *= 2
        self.dp = n * self.rp
        self.rf = ff // n
        self.ffr = up(ff // PLANE, LANES)
        self.rfp = self.ffr // self.planes
        self.slots, self.micro = slots, micro
        self.tok = slots * micro
        self.heads = HEADS * HEAD_DIM
        self.kv = KV_HEADS * HEAD_DIM
        self.qkv = self.heads + 2 * self.kv
        self.wide = self.qkv + d
        self.rv = self.kv // n


def spread_matrix(dm):
    shape = (dm.d, dm.dp)
    row, col = iota(shape, 0), iota(shape, 1)
    inner = col & (dm.rp - 1)
    hit = (row == (col // dm.rp) * dm.rows + inner) & (inner < dm.rows)
    return jnp.where(hit, 1.0, 0.0).astype(BF16)


def field_matrix(dm, offset):
    shape = (LANES, dm.dp)
    row, col = iota(shape, 0), iota(shape, 1)
    inner = col & (dm.rp - 1)
    return jnp.where((row == offset + inner) & (inner < dm.rows), 1.0, 0.0).astype(BF16)


def own_block(dm):
    shape = (dm.n, dm.dp)
    return iota(shape, 1) // dm.rp == iota(shape, 0)


def spare_rows(dm):
    shape = (dm.n, dm.dp)
    return jnp.where(iota(shape, 1) == iota(shape, 0) * dm.rp + dm.rows, 1.0, 0.0).astype(BF16)


def value_field(dm):
    shape = (LANES, LANES)
    return jnp.where(
        iota(shape, 0) == 3 * FIELD + (iota(shape, 1) & (dm.rv - 1)), 1.0, 0.0
    ).astype(BF16)


def value_block(dm):
    shape = (dm.n, LANES)
    return iota(shape, 1) // dm.rv == iota(shape, 0)


def half_turn(field):
    width = field.shape[-1]
    first = (iota(field.shape, 1) & (HEAD_DIM - 1)) < HEAD_DIM // 2
    ahead = pltpu.roll(field, width - HEAD_DIM // 2, 1)
    behind = pltpu.roll(field, HEAD_DIM // 2, 1)
    return first, ahead, behind


def twice(field):
    low = iota(field.shape, 1) < HEAD_DIM
    turned = pltpu.roll(field, HEAD_DIM, 1)
    return jnp.where(low, field, turned), jnp.where(low, turned, field)


class Refs:
    def __init__(self, names, refs):
        self.__dict__.update(zip(names, refs, strict=True))


def layer_kernel(dm, names, *refs):
    b = Refs(names, refs)
    n, planes = dm.n, dm.planes
    me = lax.axis_index("dp")
    r, p = me // PLANE, me % PLANE
    q, c = p // 2, p % 2
    other = 1 - c
    partner = r * PLANE + q * 2 + other

    def dev(plane, place):
        return (plane * PLANE + place,)

    barrier = pltpu.get_barrier_semaphore()
    peers = [dev(r, (p + k) % PLANE) for k in range(1, PLANE)]
    peers += [dev((r + k) % planes, p) for k in range(1, planes)]
    for peer in peers:
        pl.semaphore_signal(barrier, inc=1, device_id=peer, device_id_type=MESH)
    pl.semaphore_wait(barrier, len(peers))

    pending = []
    count = [0]

    def send(src, dst, arrive, to):
        copy = pltpu.make_async_remote_copy(
            src_ref=src,
            dst_ref=dst,
            send_sem=b.ssem.at[count[0]],
            recv_sem=arrive,
            device_id=to,
            device_id_type=MESH,
        )
        copy.start()
        count[0] += 1
        pending.append(copy)

    def drain():
        for copy in pending:
            copy.wait_send()
        pending.clear()

    def arrived(dst, arrive):
        pltpu.make_async_remote_copy(
            src_ref=dst,
            dst_ref=dst,
            send_sem=b.ssem.at[0],
            recv_sem=arrive,
            device_id=(partner,),
            device_id_type=MESH,
        ).wait_recv()

    def block(ref, index):
        return ref.at[index // 2, index % 2]

    def plane_rows(ref, plane):
        return ref.at[pl.ds(plane * PLANE, PLANE)]

    keep = [
        pltpu.make_async_copy(b.ap, block(b.W, me), b.csem.at[0]),
        pltpu.make_async_copy(b.gus.at[p], b.GU.at[me], b.csem.at[1]),
        pltpu.make_async_copy(b.g, b.gA.at[p], b.csem.at[2]),
    ]
    for copy in keep:
        copy.start()

    for k in range(1, planes):
        send(b.ap, block(b.W, me), b.rA.at[me], dev((r + k) % planes, p))

    def fan(index, src, k_list=(1, 2, 3)):
        for k in k_list:
            send(src, block(b.W, index), b.rA.at[index], dev(r, ((q + k) % CHIPS) * 2 + c))

    fan(me, b.ap)
    send(b.ap, block(b.W, me), b.rA.at[me], (partner,))
    for k in range(1, PLANE):
        send(b.gus.at[(p + k) % PLANE], b.GU.at[me], b.rGU.at[p], dev(r, (p + k) % PLANE))
    for k in range(1, planes):
        send(b.wds, b.WDz.at[r], b.rWZ.at[r], dev((r + k) % planes, p))

    tok = dm.tok
    xf = b.x[...].astype(F32)
    scale1 = lax.rsqrt(jnp.mean(xf * xf, axis=-1, keepdims=True) + 1e-06)
    angle = b.posc[...].astype(F32) * b.freq[...]
    b.tabs[0] = jnp.cos(angle)
    b.tabs[1] = jnp.sin(angle)
    b.spr[...] = spread_matrix(dm)

    for k in range(1, planes):
        index = ((r + planes - k) % planes) * PLANE + p
        arrived(block(b.W, index), b.rA.at[index])
        fan(index, block(b.W, index))
        send(block(b.W, index), block(b.W, index), b.rA.at[index], (partner,))
    for k in range(1, PLANE):
        origin = (p + PLANE - k) % PLANE
        arrived(b.GU.at[r * PLANE + origin], b.rGU.at[origin])
    keep[1].wait()
    for k in range(1, planes):
        send(
            plane_rows(b.GU, r),
            plane_rows(b.GU, r),
            b.rGZ.at[r],
            dev((r + k) % planes, p),
        )
    for k in range(1, CHIPS):
        for shift in range(planes):
            index = ((r + planes - shift) % planes) * PLANE + ((q + CHIPS - k) % CHIPS) * 2 + c
            arrived(block(b.W, index), b.rA.at[index])
            send(block(b.W, index), block(b.W, index), b.rA.at[index], (partner,))
    for k in range(1, CHIPS):
        send(b.g, b.gA.at[p], b.rG.at[p], dev(r, ((q + k) % CHIPS) * 2 + c))
    send(b.g, b.gA.at[p], b.rG.at[p], (partner,))

    def down_route(shift):
        origin = (r + planes - shift) % planes
        whole = origin * PLANE + p
        src = b.wds if shift == 0 else b.WDz.at[origin]
        return origin, whole // planes, whole % planes, src

    def down_copy(shift):
        origin, rank, slot, src = down_route(shift)
        return pltpu.make_async_remote_copy(
            src_ref=src,
            dst_ref=b.WD.at[slot],
            send_sem=b.wsem.at[shift],
            recv_sem=b.rWD.at[slot],
            device_id=dev(r, rank),
            device_id_type=MESH,
        )

    for shift in range(planes):
        origin, rank, slot, src = down_route(shift)
        if shift:
            arrived(b.WDz.at[origin], b.rWZ.at[origin])

        @pl.when(rank == p)
        def _():
            pltpu.make_async_copy(src, b.WD.at[slot], b.rWD.at[slot]).start()

        @pl.when(rank != p)
        def _():
            down_copy(shift).start()

    keep[0].wait()
    for k in range(CHIPS):
        for shift in range(planes):
            index = ((r + planes - shift) % planes) * PLANE + ((q + CHIPS - k) % CHIPS) * 2 + other
            arrived(block(b.W, index), b.rA.at[index])

    W = b.W.reshape(dm.dp, dm.wide)
    small = mm(spare_rows(dm), W[:, :LANES]).astype(BF16)
    mine = own_block(dm)
    rows8 = iota((8, dm.dp), 0)
    padded = jnp.zeros((8, dm.dp), F32)
    for i in range(3):
        piece = mm(small, field_matrix(dm, i * FIELD))
        piece = jnp.sum(jnp.where(mine, piece, 0.0), axis=0, keepdims=True)
        padded = jnp.where(rows8 == i, piece, padded)
    b.vec[...] = mm_nt(padded.astype(BF16), b.spr[...])
    gain1, bias_q, gain2 = b.vec[0:1], b.vec[1:2], b.vec[2:3]
    bias_v = jnp.sum(
        jnp.where(value_block(dm), mm(small, value_field(dm)), 0.0), axis=0, keepdims=True
    )
    bias_k = b.bkey[...].astype(F32)

    normed = (xf * scale1 * gain1).astype(BF16)
    b.npad[...] = mm(normed, b.spr[...]).astype(BF16)
    lin = mm(b.npad[...], W[:, : dm.qkv])
    turn_in = jnp.concatenate([lin[:, : dm.heads] + bias_q, lin[:, dm.heads : dm.heads + dm.kv] + bias_k], axis=1)
    reps = (dm.heads + dm.kv) // LANES
    cosine = jnp.concatenate([b.tabs[0]] * reps, axis=1)
    sine = jnp.concatenate([b.tabs[1]] * reps, axis=1)
    first, ahead, behind = half_turn(turn_in)
    turned = turn_in * cosine + jnp.where(first, -ahead, behind) * sine
    values = lin[:, dm.heads + dm.kv :] + bias_v
    for i, piece in enumerate(twice(turned[:, dm.heads :])):
        b.kd[i] = piece.astype(BF16)
    for i, piece in enumerate(twice(values)):
        b.vd[i] = piece.astype(BF16)
    low = iota((dm.slots, LANES), 1) < HEAD_DIM

    def stack_heads(field, store):
        for h in range(HEADS):
            part = field[:, LANES * (h // 2) : LANES * (h // 2) + LANES]
            part = jnp.where(low if h % 2 == 0 else ~low, part, 0.0)
            store[h * dm.slots : (h + 1) * dm.slots, :] = part.astype(BF16)

    span = GROUP * dm.slots
    for m in range(dm.micro):
        here = slice(m * dm.slots, (m + 1) * dm.slots)
        stack_heads(turned[here, : dm.heads], b.QS.at[m])
        grid = (dm.slots, dm.slots)
        start_row = iota((dm.slots, 1), 0) - b.posc[here]
        start_col = iota((1, dm.slots), 1) - b.posr[m : m + 1]
        allowed = (start_row == start_col) & (iota(grid, 1) <= iota(grid, 0))
        for kv in range(KV_HEADS):
            rows = slice(kv * span, (kv + 1) * span)
            score = mm_nt(b.QS[m, rows], b.kd[kv, here]) * 0.125
            score = jnp.where(allowed[None], score.reshape(GROUP, *grid), -1e30)
            top = jnp.max(score, axis=-1, keepdims=True)
            expo = jnp.exp(score - top)
            prob = expo / jnp.sum(expo, axis=-1, keepdims=True)
            prob = prob.reshape(span, dm.slots)
            b.PF[m, rows] = prob
            b.DMS[rows] = mm(prob.astype(BF16), b.vd[kv, here]).astype(BF16)
        for t in range(HEADS // 2):
            even = b.DMS[2 * t * dm.slots : (2 * t + 1) * dm.slots]
            odd = b.DMS[(2 * t + 1) * dm.slots : (2 * t + 2) * dm.slots]
            b.mix[here, t * LANES : (t + 1) * LANES] = jnp.where(low, even, odd)
    b.mpad[...] = mm(b.mix[...], b.spr[...]).astype(BF16)
    hidden = xf + mm(b.mpad[...], W[:, dm.qkv :])
    b.hid[...] = hidden
    scale2 = lax.rsqrt(jnp.mean(hidden * hidden, axis=-1, keepdims=True) + 1e-06)
    nf = (hidden * scale2 * gain2).astype(BF16)
    b.nfA[p] = mm(nf, b.spr[...]).astype(BF16)

    for k in range(1, CHIPS):
        send(b.nfA.at[p], b.nfA.at[p], b.rNF.at[p], dev(r, ((q + k) % CHIPS) * 2 + c))
    send(b.nfA.at[p], b.nfA.at[p], b.rNF.at[p], (partner,))
    for k in range(1, CHIPS):
        place = ((q + CHIPS - k) % CHIPS) * 2 + c
        arrived(b.gA.at[place], b.rG.at[place])
        send(b.gA.at[place], b.gA.at[place], b.rG.at[place], (partner,))
    for k in range(1, CHIPS):
        place = ((q + CHIPS - k) % CHIPS) * 2 + c
        arrived(b.nfA.at[place], b.rNF.at[place])
        send(b.nfA.at[place], b.nfA.at[place], b.rNF.at[place], (partner,))
    for k in range(1, planes):
        origin = (r + planes - k) % planes
        arrived(plane_rows(b.GU, origin), b.rGZ.at[origin])
    for slot in range(planes):
        arrived(b.WD.at[slot], b.rWD.at[slot])
    keep[2].wait()
    for k in range(CHIPS):
        place = ((q + CHIPS - k) % CHIPS) * 2 + other
        arrived(b.gA.at[place], b.rG.at[place])
        arrived(b.nfA.at[place], b.rNF.at[place])

    GU = b.GU.reshape(dm.dp, 2 * dm.ffr)
    WD = b.WD.reshape(dm.ffr, dm.d)
    BIG = b.BIG.reshape(dm.dp, 4 * dm.ffr)
    half = PLANE // 2

    def feed(place_q, place_c, slot):
        place = place_q * 2 + place_c
        nf_t, g_t = b.nfA[place], b.gA[place]
        pre = mm(nf_t, GU[...])
        gate, upper = pre[:, : dm.ffr], pre[:, dm.ffr :]
        sigma = jax.nn.sigmoid(gate)
        silu = gate * sigma
        act = (silu * upper).astype(BF16)
        b.act[pl.ds(pl.multiple_of(place * tok, tok), tok), :] = act
        b.oP[place_q, place_c] = mm(act, WD[...]).astype(BF16)
        d_act = mm_nt(g_t, WD[...])
        d_gate = (d_act * upper * (sigma + silu * (1.0 - sigma))).astype(BF16)
        d_up = (d_act * silu).astype(BF16)
        d_both = jnp.concatenate([d_gate, d_up], axis=1)
        rows = pl.ds(pl.multiple_of((place % half) * tok, tok), tok)
        cols = pl.ds(pl.multiple_of((place // half) * 2 * dm.ffr, LANES), 2 * dm.ffr)
        BIG[rows, cols] = d_both
        b.dP[place_q, place_c] = mm_nt(d_both, GU[...]).astype(BF16)

    def first_copy(where, part, landing, sems, arrive):
        return pltpu.make_async_remote_copy(
            src_ref=part.at[where, other],
            dst_ref=landing.at[where],
            send_sem=sems.at[where],
            recv_sem=arrive.at[where],
            device_id=(partner,),
            device_id_type=MESH,
        )

    @pl.loop(0, CHIPS)
    def _(step):
        where = (q + step) % CHIPS

        @pl.loop(0, 2)
        def _(turn):
            feed(where, (other + turn) % 2, step)

            @pl.when(turn == 0)
            def _():
                first_copy(where, b.oP, b.oR1, b.osem, b.rO1).start()
                first_copy(where, b.dP, b.dR1, b.dsem, b.rD1).start()

    for k in (1, 2, 3, 0):
        where = (q + k) % CHIPS
        arrived(b.oR1.at[where], b.rO1.at[where])
        b.oP[where, c] = (b.oP[where, c].astype(F32) + b.oR1[where].astype(F32)).astype(BF16)
        arrived(b.dR1.at[where], b.rD1.at[where])
        b.dP[where, c] = (b.dP[where, c].astype(F32) + b.dR1[where].astype(F32)).astype(BF16)
        if k:
            send(b.dP.at[where, c], b.dR2.at[k - 1], b.rD2.at[k - 1], dev(r, where * 2 + c))
            send(b.oP.at[where, c], b.oR2.at[k - 1], b.rO2.at[k - 1], dev(r, where * 2 + c))

    for shift in range(planes):
        origin, rank, slot, src = down_route(shift)

        @pl.when(rank != p)
        def _():
            down_copy(shift).wait_send()

    drain()
    nf_all = b.nfA.reshape(PLANE * tok, dm.dp)
    g_all = b.gA.reshape(PLANE * tok, dm.d)
    wide_rows = dm.dp
    chunk = dm.dp // 4

    @pl.loop(0, 4)
    def _(i):
        cols = pl.ds(pl.multiple_of(i * chunk, chunk), chunk)
        total = mm_tn(nf_all[:wide_rows, cols], BIG[:, : 2 * dm.ffr])
        total = total + mm_tn(nf_all[wide_rows:, cols], BIG[:, 2 * dm.ffr :])
        GU[cols, :] = total.astype(BF16)

    for k in range(1, planes):
        to = (r + k) % planes
        send(plane_rows(b.GU, to), b.zR.at[k - 1], b.rZ.at[k - 1], dev(to, p))
    WD[...] = mm_tn(b.act[...], g_all[...]).astype(BF16)

    def down_back(slot):
        whole = p * planes + slot
        return whole // PLANE, whole % PLANE

    def down_back_copy(slot):
        plane_to, place_to = down_back(slot)
        return pltpu.make_async_remote_copy(
            src_ref=b.WD.at[slot],
            dst_ref=b.dWDz.at[plane_to],
            send_sem=b.vsem.at[slot],
            recv_sem=b.rW1.at[plane_to],
            device_id=dev(r, place_to),
            device_id_type=MESH,
        )

    for slot in range(planes):
        plane_to, place_to = down_back(slot)

        @pl.when(place_to == p)
        def _():
            pltpu.make_async_copy(b.WD.at[slot], b.dWDz.at[plane_to], b.rW1.at[plane_to]).start()

        @pl.when(place_to != p)
        def _():
            down_back_copy(slot).start()

    d_nf = b.dP[q, c].astype(F32)
    total = b.oP[q, c].astype(F32)
    for k in range(1, CHIPS):
        arrived(b.dR2.at[k - 1], b.rD2.at[k - 1])
        d_nf = d_nf + b.dR2[k - 1].astype(F32)
    for k in range(1, CHIPS):
        arrived(b.oR2.at[k - 1], b.rO2.at[k - 1])
        total = total + b.oR2[k - 1].astype(F32)
    hidden = b.hid[...]
    b.out[...] = (hidden + total).astype(BF16)
    d_nf = split_mm(d_nf, b.spr[...], nt=True)
    scale2 = lax.rsqrt(jnp.mean(hidden * hidden, axis=-1, keepdims=True) + 1e-06)

    def norm_back(grad, field, scale, gain):
        weighted = grad * gain
        d_gain = jnp.sum(grad * field * scale, axis=0, keepdims=True)
        d_field = weighted * scale - field * (scale * scale * scale) * jnp.mean(
            weighted * field, axis=-1, keepdims=True
        )
        return d_gain, d_field

    d_gain2, d_part = norm_back(d_nf, hidden, scale2, b.vec[2:3])
    d_hidden = b.g[...].astype(F32) + d_part
    b.hid[...] = d_hidden
    d_attn = d_hidden.astype(BF16)
    for k in range(1, planes):
        to = (r + k) % planes
        arrived(b.dWDz.at[to], b.rW1.at[to])
        send(b.dWDz.at[to], b.dWDr.at[k - 1], b.rW2.at[k - 1], dev(to, p))

    BIG[:, dm.qkv : dm.wide] = mm_tn(b.mpad[...], d_attn).astype(BF16)
    d_mixed = mm_nt(d_attn, W[:, dm.qkv :]).astype(BF16)
    d_mixed = mm_nt(d_mixed, b.spr[...])
    d_values = []
    for m in range(dm.micro):
        here = slice(m * dm.slots, (m + 1) * dm.slots)
        stack_heads(d_mixed[here], b.DMS)
        d_v, d_k = [], []
        for kv in range(KV_HEADS):
            rows = slice(kv * span, (kv + 1) * span)
            dms, prob, qs = b.DMS[rows], b.PF[m, rows], b.QS[m, rows]
            d_v.append(mm_tn(prob.astype(BF16), dms))
            d_prob = mm_nt(dms, b.vd[kv, here])
            delta = jnp.sum(d_prob * prob, axis=-1, keepdims=True)
            d_score = (prob * (d_prob - delta)).astype(BF16)
            d_k.append(0.125 * mm_tn(d_score, qs))
            b.PF[m, rows] = 0.125 * mm(d_score, b.kd[kv, here])
        for t in range(HEADS // 2):
            even = b.PF[m, 2 * t * dm.slots : (2 * t + 1) * dm.slots]
            odd = b.PF[m, (2 * t + 1) * dm.slots : (2 * t + 2) * dm.slots]
            b.FQ[here, t * LANES : (t + 1) * LANES] = jnp.where(low, even, odd)

        def joined(pair):
            zero, one = (piece + pltpu.roll(piece, HEAD_DIM, 1) for piece in pair)
            return jnp.where(low, zero, one)

        b.FQ[here, dm.heads : dm.heads + dm.kv] = joined(d_k)
        d_values.append(joined(d_v))
    d_turned = b.FQ[...]
    cosine = jnp.concatenate([b.tabs[0]] * reps, axis=1)
    sine = jnp.concatenate([b.tabs[1]] * reps, axis=1)
    first, ahead, behind = half_turn(d_turned * sine)
    d_lin = (d_turned * cosine + jnp.where(first, ahead, -behind)).astype(BF16)
    d_lin = jnp.concatenate([d_lin, jnp.concatenate(d_values, axis=0).astype(BF16)], axis=1)
    BIG[:, : dm.qkv] = mm_tn(b.npad[...], d_lin).astype(BF16)
    d_bias = jnp.sum(d_lin.astype(F32), axis=0, keepdims=True)
    d_normed = split_mm(mm_nt(d_lin, W[:, : dm.qkv]), b.spr[...], nt=True)
    xf = b.x[...].astype(F32)
    scale1 = lax.rsqrt(jnp.mean(xf * xf, axis=-1, keepdims=True) + 1e-06)
    d_gain1, d_part = norm_back(d_normed, xf, scale1, b.vec[0:1])
    b.gin[...] = (b.hid[...] + d_part).astype(BF16)

    rows8 = iota((8, dm.d), 0)
    packed = jnp.zeros((8, dm.d), F32)
    for i, piece in enumerate((d_gain1, d_bias[:, : dm.heads], d_gain2)):
        packed = jnp.where(rows8 == i, piece, packed)
    packed = split_mm(packed, b.spr[...])
    mine = own_block(dm)
    spare = jnp.zeros((n, LANES), F32)
    for i in range(3):
        piece = jnp.where(mine, packed[i : i + 1], 0.0).astype(BF16)
        spare = spare + mm_nt(piece, field_matrix(dm, i * FIELD))
    piece = jnp.where(value_block(dm), d_bias[:, dm.heads + dm.kv :], 0.0).astype(BF16)
    spare = spare + mm_nt(piece, value_field(dm))
    key_bias = jnp.broadcast_to(d_bias[:, dm.heads : dm.heads + dm.kv], (n, LANES))
    spare = jnp.concatenate([spare, key_bias], axis=1).astype(BF16)
    BIG[:, : 2 * LANES] = (
        BIG[:, : 2 * LANES].astype(F32) + mm_tn(spare_rows(dm), spare)
    ).astype(BF16)

    cols = pl.ds(0, dm.wide)

    def quad(plane):
        return pl.ds(plane * CHIPS, CHIPS)

    for k in (*range(1, planes), 0):
        to = (r + k) % planes
        send(b.BIG.at[quad(to), other, :, cols], b.aR1.at[quad(to)], b.rA1.at[to], (partner,))
    for k in (*range(1, planes), 0):
        to = (r + k) % planes
        arrived(b.aR1.at[quad(to)], b.rA1.at[to])
        mine_now = b.BIG[quad(to), c, :, cols].astype(F32) + b.aR1[quad(to)].astype(F32)
        b.aR1[quad(to)] = mine_now.astype(BF16)
        for j in range(1, CHIPS):
            where = (q + j) % CHIPS
            send(
                b.aR1.at[to * CHIPS + where],
                b.aR2.at[j - 1, to],
                b.rA2.at[j - 1, to],
                dev(r, where * 2 + c),
            )
    mine_gu = plane_rows(b.GU, r)
    total = mine_gu[...].astype(F32)
    for k in range(1, planes):
        arrived(b.zR.at[k - 1], b.rZ.at[k - 1])
        total = total + b.zR[k - 1].astype(F32)
    mine_gu[...] = total.astype(BF16)
    for k in range(1, PLANE):
        to = (p + k) % PLANE
        send(b.GU.at[r * PLANE + to], b.fgu.at[p], b.rF.at[p], dev(r, to))
    b.fgu[p] = b.GU[me]
    for k in (*range(1, planes), 0):
        to = (r + k) % planes
        total = b.aR1[to * CHIPS + q].astype(F32)
        for j in range(1, CHIPS):
            arrived(b.aR2.at[j - 1, to], b.rA2.at[j - 1, to])
            total = total + b.aR2[j - 1, to].astype(F32)
        if k:
            b.aR2[0, to] = total.astype(BF16)
            send(b.aR2.at[0, to], b.aR3.at[k - 1], b.rA3.at[k - 1], dev(to, p))
    arrived(b.dWDz.at[r], b.rW1.at[r])
    down = b.dWDz[r].astype(F32)
    for k in range(1, planes):
        arrived(b.dWDr.at[k - 1], b.rW2.at[k - 1])
        down = down + b.dWDr[k - 1].astype(F32)
    b.fwd[...] = down
    for k in range(1, planes):
        arrived(b.aR3.at[k - 1], b.rA3.at[k - 1])
        total = total + b.aR3[k - 1].astype(F32)
    b.fa[...] = total
    for k in range(1, PLANE):
        origin = (p + PLANE - k) % PLANE
        arrived(b.fgu.at[origin], b.rF.at[origin])
    for slot in range(planes):
        plane_to, place_to = down_back(slot)

        @pl.when(place_to != p)
        def _():
            down_back_copy(slot).wait_send()

    for where in range(CHIPS):
        first_copy(where, b.oP, b.oR1, b.osem, b.rO1).wait_send()
        first_copy(where, b.dP, b.dR1, b.dsem, b.rD1).wait_send()
    drain()


def run_layer(dm, operands):
    n, planes, rp, tok = dm.n, dm.planes, dm.rp, dm.tok
    vm = pltpu.VMEM
    sem = pltpu.SemaphoreType.DMA
    quads = planes * CHIPS
    pairs = dm.heads + dm.kv
    outs = {
        "out": jax.ShapeDtypeStruct((tok, dm.d), BF16),
        "gin": jax.ShapeDtypeStruct((tok, dm.d), BF16),
        "fa": jax.ShapeDtypeStruct((rp, dm.wide), F32),
        "fgu": jax.ShapeDtypeStruct((PLANE, rp, 2 * dm.ffr), BF16),
        "fwd": jax.ShapeDtypeStruct((dm.rfp, dm.d), F32),
    }
    n_sends = 1 + (planes - 1) * 5 + 8 * PLANE + 8 * quads + 64
    scratch = {
        "W": vm((quads, 2, rp, dm.wide), BF16),
        "GU": vm((n, rp, 2 * dm.ffr), BF16),
        "WDz": vm((planes, dm.rfp, dm.d), BF16),
        "WD": vm((planes, dm.rfp, dm.d), BF16),
        "nfA": vm((PLANE, tok, dm.dp), BF16),
        "gA": vm((PLANE, tok, dm.d), BF16),
        "act": vm((PLANE * tok, dm.ffr), BF16),
        "BIG": vm((quads, 2, rp, 4 * dm.ffr), BF16),
        "oP": vm((CHIPS, 2, tok, dm.d), BF16),
        "dP": vm((CHIPS, 2, tok, dm.dp), BF16),
        "oR1": vm((CHIPS, tok, dm.d), BF16),
        "dR1": vm((CHIPS, tok, dm.dp), BF16),
        "oR2": vm((CHIPS - 1, tok, dm.d), BF16),
        "dR2": vm((CHIPS - 1, tok, dm.dp), BF16),
        "zR": vm((planes - 1, PLANE, rp, 2 * dm.ffr), BF16),
        "dWDz": vm((planes, dm.rfp, dm.d), BF16),
        "dWDr": vm((planes - 1, dm.rfp, dm.d), BF16),
        "aR1": vm((quads, rp, dm.wide), BF16),
        "aR2": vm((CHIPS - 1, planes, rp, dm.wide), BF16),
        "aR3": vm((planes - 1, rp, dm.wide), BF16),
        "QS": vm((dm.micro, HEADS * dm.slots, LANES), BF16),
        "PF": vm((dm.micro, HEADS * dm.slots, dm.slots), F32),
        "DMS": vm((HEADS * dm.slots, LANES), BF16),
        "hid": vm((tok, dm.d), F32),
        "npad": vm((tok, dm.dp), BF16),
        "mpad": vm((tok, dm.dp), BF16),
        "spr": vm((dm.d, dm.dp), BF16),
        "kd": vm((KV_HEADS, tok, LANES), BF16),
        "vd": vm((KV_HEADS, tok, LANES), BF16),
        "FQ": vm((tok, pairs), F32),
        "mix": vm((tok, dm.d), BF16),
        "tabs": vm((2, tok, LANES), F32),
        "vec": vm((8, dm.d), F32),
        "ssem": sem((n_sends,)),
        "csem": sem((3,)),
        "osem": sem((CHIPS,)),
        "dsem": sem((CHIPS,)),
        "wsem": sem((planes,)),
        "vsem": sem((planes,)),
        "rA": sem((n,)),
        "rGU": sem((PLANE,)),
        "rGZ": sem((planes,)),
        "rG": sem((PLANE,)),
        "rWZ": sem((planes,)),
        "rWD": sem((planes,)),
        "rNF": sem((PLANE,)),
        "rO1": sem((CHIPS,)),
        "rD1": sem((CHIPS,)),
        "rO2": sem((CHIPS - 1,)),
        "rD2": sem((CHIPS - 1,)),
        "rZ": sem((planes - 1,)),
        "rF": sem((PLANE,)),
        "rW1": sem((planes,)),
        "rW2": sem((planes - 1,)),
        "rA1": sem((planes,)),
        "rA2": sem((CHIPS - 1, planes)),
        "rA3": sem((planes - 1,)),
    }
    return pl.pallas_call(
        functools.partial(layer_kernel, dm, (*operands, *outs, *scratch)),
        name="layer",
        out_shape=list(outs.values()),
        in_specs=[pl.BlockSpec(memory_space=pltpu.VMEM)] * len(operands),
        out_specs=[pl.BlockSpec(memory_space=pltpu.VMEM)] * len(outs),
        scratch_shapes=list(scratch.values()),
        compiler_params=pltpu.CompilerParams(
            collective_id=0, has_side_effects=True, vmem_limit_bytes=67043328
        ),
    )(*operands.values())


def per_device(n, *args):
    (
        tokens,
        positions,
        cotangent,
        norm_attn,
        w_query,
        b_query,
        w_key,
        b_key,
        w_value,
        b_value,
        w_out,
        norm_ffn,
        w_gate,
        w_up,
        w_down,
    ) = args
    micro, slots, d = tokens.shape
    dm = Dims(n, d, w_gate.shape[0] * n // d, slots, micro)
    rows, rp = dm.rows, dm.rp

    def lanes(vector):
        return jnp.pad(vector, (0, FIELD - vector.shape[0]))

    spare = jnp.concatenate([lanes(v) for v in (norm_attn, b_query, norm_ffn, b_value)])
    spare = jnp.pad(spare, (0, dm.wide - spare.shape[0]))
    pack = jnp.concatenate(
        [w.reshape(rows, -1) for w in (w_query, w_key, w_value, w_out)], axis=1
    )
    pack = jnp.concatenate([pack, spare[None]], axis=0)
    pack = jnp.pad(pack, ((0, rp - rows - 1), (0, 0)))

    def columns(weight):
        weight = weight.reshape(rows, PLANE, dm.planes, dm.rf)
        weight = jnp.pad(weight, ((0, rp - rows), (0, 0), (0, 0), (0, dm.rfp - dm.rf)))
        return weight.reshape(rp, PLANE, dm.ffr)

    both = jnp.concatenate([columns(w_gate), columns(w_up)], axis=2)
    both = both.transpose(1, 0, 2)
    down = jnp.pad(w_down.reshape(dm.rf, d), ((0, dm.rfp - dm.rf), (0, 0)))
    half_dim = HEAD_DIM // 2
    freq = 1000000.0 ** (-(jnp.arange(half_dim).astype(F32) * 2.0 / HEAD_DIM))
    freq = jnp.tile(freq, LANES // half_dim)[None]
    operands = {
        "x": tokens.reshape(dm.tok, d),
        "g": cotangent.reshape(dm.tok, d),
        "posc": positions.reshape(dm.tok, 1),
        "posr": positions,
        "freq": freq,
        "bkey": b_key[None],
        "ap": pack,
        "gus": both,
        "wds": down,
    }
    out, gin, fa, fgu, fwd = run_layer(dm, operands)

    def field(i, size):
        return fa[rows, i * FIELD : i * FIELD + size]

    def flat(start, stop):
        return fa[:rows, start:stop].reshape(-1)

    def gate_part(start):
        part = fgu[:, :rows, start : start + dm.ffr].astype(F32)
        part = part.reshape(PLANE, rows, dm.planes, dm.rfp)[..., : dm.rf]
        return part.transpose(1, 0, 2, 3).reshape(-1)

    h, kv = dm.heads, dm.kv
    return (
        out.reshape(micro, slots, d),
        gin.reshape(micro, slots, d),
        field(0, rows),
        flat(0, h),
        field(1, rows),
        flat(h, h + kv),
        fa[rows, LANES : LANES + kv],
        flat(h + kv, h + 2 * kv),
        field(3, dm.rv),
        flat(h + 2 * kv, dm.wide),
        field(2, rows),
        gate_part(0),
        gate_part(dm.ffr),
        fwd[: dm.rf].reshape(-1),
    )


def solution(mesh):
    n = mesh.shape["dp"]
    split, row = P("dp"), P(None, "dp", None)
    in_specs = (row, P(None, "dp"), row, *[split] * 4, P(), *[split] * 7)
    out_specs = (row, row, *[split] * 4, P(), *[split] * 7)
    return jax.shard_map(
        functools.partial(per_device, n),
        mesh=mesh,
        in_specs=in_specs,
        out_specs=out_specs,
        check_vma=False,
    )
```

time: 1450 us -> 308 us (0.21)
  the two profiles are of different devices: /device:TPU:0 before, /device:TPU:28 now
where the time goes in v1:
time: 308 us; the launch traced here: 307 us
  Pallas kernels  277 us (90%)
  local copies, waits for them, and re-layouts  25.3 us (8%)
  other arithmetic  3.39 us (1%)
    pallas_call x1, Pallas kernels, run_layer(): pl.pallas_call(functools.partial(layer_kernel, dm, (*operands, *outs, *sc...  277 us

profile of v1, /device:TPU:28, one launch (start us, length us, event | category | flops | bytes accessed | tf_op | source)
XLA Modules:
  0.0 306.9 jit_solution(15412112944461621092)
XLA Ops:
  0.7 0.8 fusion.11
  1.5 0.6 broadcast_in_dim_tile.3.refs_4_
  2.1 0.9 reshape.115
  3.0 0.9 reshape.118
  3.9 1.4 fusion.8.refs_6_
  5.3 1.5 copy.31.refs_2_
  6.8 1.2 reshape.123
  8.0 0.7 pad.41.refs_8_
  8.7 1.3 reshape.119
  11.3 1.3 reshape.121
  13.3 0.9 maximum_bitcast_fusion.refs_7_
  14.2 277.4 %layer.1 = (bf16[256,896]{1,0:T(8,128)(2,1)}, bf16[256,896]{1,0:T(8,128)(2,1)}, f32[32,2048]{1,0:T(8,128)}, bf16[8,32,1280]{2,1,0:T(8,128)(2,1)}, f32[160,896]{1,0:T(8,128)}) custom-call(bf16[256,896]{1,0:T(8,128)(2,1)} %bitcast.32, bf16[256,896]{1,0:T(8,128)(2,1)} %bitcast.33, s32[256,1]{1,0:T(8,128)} %copy.31.refs_2_, s32[2,128]{1,0:T(2,128)} %refs_3_.1, ...), custom_call_target="tpu_custom_call" | custom-call | tf_op jit(solution)/shard_map/layer/pallas_call | solution.py:700
  291.6 1.3 slice_bitcast_fusion.4
  292.9 1.3 slice_bitcast_fusion.3
  294.1 1.4 slice_bitcast_fusion.2
  295.5 1.3 slice_bitcast_fusion
  296.9 1.0 fusion.13
  297.8 0.7 reshape.129
  298.5 0.7 reshape.126
  299.2 0.8 reshape.136
  301.5 1.9 reshape.138
  303.5 1.9 reshape.140
  305.4 0.8 copy.38
  306.2 0.8 copy.39
  (30 shorter events, 3.4 us)
Async XLA Ops:
  0.6 8.1 %copy-start.4 = (bf16[136192]{0:T(1024)(128)(2,1)S(1)}, bf16[136192]{0:T(1024)(128)(2,1)}, u32[]{:S(2)}) copy-start(bf16[136192]{0:T(1024)(128)(2,1)} %param.27) | copy-start | bytes 817156
  10.4 1.0 copy-start.5
  291.6 7.5 %copy-start.1 = (f32[160,896]{1,0:T(8,128)S(1)}, f32[160,896]{1,0:T(8,128)}, u32[]{:S(2)}) copy-start(f32[160,896]{1,0:T(8,128)} %get-tuple-element.23) | copy-start | bytes 1720324
  299.1 1.3 copy-start
  303.5 1.9 copy-start.3
  303.5 2.7 copy-start.2

commit v2 on v1

--- a/solution.py
+++ b/solution.py
@@ -66,6 +66,9 @@
         self.qkv = self.heads + 2 * self.kv
         self.wide = self.qkv + d
         self.rv = self.kv // n
+        self.unit = PLANE * self.rows
+        self.gs = 16 if self.unit % 16 == 0 else 8
+        self.groups = self.unit // self.gs
 
 
 def spread_matrix(dm):
@@ -126,7 +129,7 @@
 
 def layer_kernel(dm, names, *refs):
     b = Refs(names, refs)
-    n, planes = dm.n, dm.planes
+    n, planes, rp = dm.n, dm.planes, dm.rp
     me = lax.axis_index("dp")
     r, p = me // PLANE, me % PLANE
     q, c = p // 2, p % 2
@@ -146,7 +149,7 @@
     pending = []
     count = [0]
 
-    def send(src, dst, arrive, to):
+    def send(src, dst, arrive, to, cond=None):
         copy = pltpu.make_async_remote_copy(
             src_ref=src,
             dst_ref=dst,
@@ -155,14 +158,35 @@
             device_id=to,
             device_id_type=MESH,
         )
-        copy.start()
         count[0] += 1
-        pending.append(copy)
-
-    def drain():
-        for copy in pending:
-            copy.wait_send()
-        pending.clear()
+        pending.append((copy, cond))
+        if cond is None:
+            copy.start()
+        else:
+            pl.when(cond)(copy.start)
+
+    def drain(left=0):
+        for copy, cond in pending[: len(pending) - left]:
+            if cond is None:
+                copy.wait_send()
+            else:
+                pl.when(cond)(copy.wait_send)
+        del pending[: len(pending) - left]
+
+    upper = r // max(planes // 2, 1)
+    mirror = r + upper * (planes - 1 - 2 * r)
+
+    def origin_of(k):
+        spot = k - (mirror + planes - k) // planes
+        return spot + upper * (planes - 1 - 2 * spot)
+
+    def relay(src, dst, arrive, origin=None):
+        if origin is None:
+            send(src, dst, arrive, dev(r + 1, p), r + 1 < planes)
+            send(src, dst, arrive, dev(r - 1, p), r >= 1)
+        else:
+            to = r - 1 + 2 * ((r - origin - 1 + planes) // planes)
+            send(src, dst, arrive, dev(to, p), (to >= 0) & (to < planes))
 
     def arrived(dst, arrive):
         pltpu.make_async_remote_copy(
@@ -178,18 +202,18 @@
         return ref.at[index // 2, index % 2]
 
     def plane_rows(ref, plane):
-        return ref.at[pl.ds(plane * PLANE, PLANE)]
+        return ref.at[pl.ds(plane * dm.groups, dm.groups)]
 
     keep = [
         pltpu.make_async_copy(b.ap, block(b.W, me), b.csem.at[0]),
-        pltpu.make_async_copy(b.gus.at[p], b.GU.at[me], b.csem.at[1]),
+        pltpu.make_async_copy(b.gus.at[p], b.fgu.at[p], b.csem.at[1]),
         pltpu.make_async_copy(b.g, b.gA.at[p], b.csem.at[2]),
+        pltpu.make_async_copy(b.wds, b.WD.at[r], b.csem.at[3]),
     ]
     for copy in keep:
         copy.start()
 
-    for k in range(1, planes):
-        send(b.ap, block(b.W, me), b.rA.at[me], dev((r + k) % planes, p))
+    relay(b.ap, block(b.W, me), b.rA.at[me])
 
     def fan(index, src, k_list=(1, 2, 3)):
         for k in k_list:
@@ -198,9 +222,8 @@
     fan(me, b.ap)
     send(b.ap, block(b.W, me), b.rA.at[me], (partner,))
     for k in range(1, PLANE):
-        send(b.gus.at[(p + k) % PLANE], b.GU.at[me], b.rGU.at[p], dev(r, (p + k) % PLANE))
-    for k in range(1, planes):
-        send(b.wds, b.WDz.at[r], b.rWZ.at[r], dev((r + k) % planes, p))
+        send(b.gus.at[(p + k) % PLANE], b.fgu.at[p], b.rGU.at[p], dev(r, (p + k) % PLANE))
+    relay(b.wds, b.WD.at[r], b.rWD.at[r])
 
     tok = dm.tok
     xf = b.x[...].astype(F32)
@@ -211,21 +234,35 @@
     b.spr[...] = spread_matrix(dm)
 
     for k in range(1, planes):
-        index = ((r + planes - k) % planes) * PLANE + p
+        origin = origin_of(k)
+        index = origin * PLANE + p
         arrived(block(b.W, index), b.rA.at[index])
+        relay(block(b.W, index), block(b.W, index), b.rA.at[index], origin)
         fan(index, block(b.W, index))
         send(block(b.W, index), block(b.W, index), b.rA.at[index], (partner,))
     for k in range(1, PLANE):
         origin = (p + PLANE - k) % PLANE
-        arrived(b.GU.at[r * PLANE + origin], b.rGU.at[origin])
+        arrived(b.fgu.at[origin], b.rGU.at[origin])
     keep[1].wait()
-    for k in range(1, planes):
-        send(
-            plane_rows(b.GU, r),
-            plane_rows(b.GU, r),
-            b.rGZ.at[r],
-            dev((r + k) % planes, p),
-        )
+    GU = b.GU.reshape(dm.d, 2 * dm.ffr)
+    my_rows = pl.ds(pl.multiple_of(r * dm.unit, dm.gs), dm.unit)
+    squeeze = b.spr[: dm.unit, : PLANE * rp]
+    for i in range(2):
+        piece = b.fgu[:, i].reshape(PLANE * rp, dm.ffr)
+        GU[my_rows, i * dm.ffr : (i + 1) * dm.ffr] = mm(squeeze, piece).astype(BF16)
+    relay(plane_rows(b.GU, r), plane_rows(b.GU, r), b.rGZ.at[r])
+
+    def relay_down(k):
+        origin = origin_of(k)
+        arrived(b.WD.at[origin], b.rWD.at[origin])
+        relay(b.WD.at[origin], b.WD.at[origin], b.rWD.at[origin], origin)
+
+    def relay_gate(k):
+        origin = origin_of(k)
+        arrived(plane_rows(b.GU, origin), b.rGZ.at[origin])
+        relay(plane_rows(b.GU, origin), plane_rows(b.GU, origin), b.rGZ.at[origin], origin)
+
+    relay_down(1)
     for k in range(1, CHIPS):
         for shift in range(planes):
             index = ((r + planes - shift) % planes) * PLANE + ((q + CHIPS - k) % CHIPS) * 2 + c
@@ -235,35 +272,8 @@
         send(b.g, b.gA.at[p], b.rG.at[p], dev(r, ((q + k) % CHIPS) * 2 + c))
     send(b.g, b.gA.at[p], b.rG.at[p], (partner,))
 
-    def down_route(shift):
-        origin = (r + planes - shift) % planes
-        whole = origin * PLANE + p
-        src = b.wds if shift == 0 else b.WDz.at[origin]
-        return origin, whole // planes, whole % planes, src
-
-    def down_copy(shift):
-        origin, rank, slot, src = down_route(shift)
-        return pltpu.make_async_remote_copy(
-            src_ref=src,
-            dst_ref=b.WD.at[slot],
-            send_sem=b.wsem.at[shift],
-            recv_sem=b.rWD.at[slot],
-            device_id=dev(r, rank),
-            device_id_type=MESH,
-        )
-
-    for shift in range(planes):
-        origin, rank, slot, src = down_route(shift)
-        if shift:
-            arrived(b.WDz.at[origin], b.rWZ.at[origin])
-
-        @pl.when(rank == p)
-        def _():
-            pltpu.make_async_copy(src, b.WD.at[slot], b.rWD.at[slot]).start()
-
-        @pl.when(rank != p)
-        def _():
-            down_copy(shift).start()
+    for k in range(2, min(planes, 3)):
+        relay_down(k)
 
     keep[0].wait()
     for k in range(CHIPS):
@@ -307,12 +317,19 @@
         for h in range(HEADS):
             part = field[:, LANES * (h // 2) : LANES * (h // 2) + LANES]
             part = jnp.where(low if h % 2 == 0 else ~low, part, 0.0)
-            store[h * dm.slots : (h + 1) * dm.slots, :] = part.astype(BF16)
+            store(h)[...] = part.astype(BF16)
 
     span = GROUP * dm.slots
+    mix = b.oP.at[0, 0]
+    BIG = b.BIG.reshape(dm.dp, 4 * dm.ffr)
+    dms = [BIG.at[:span, dm.wide + kv * LANES : dm.wide + (kv + 1) * LANES] for kv in range(KV_HEADS)]
+
+    def head_rows(h):
+        return dms[h // GROUP].at[(h % GROUP) * dm.slots : (h % GROUP + 1) * dm.slots]
+
     for m in range(dm.micro):
         here = slice(m * dm.slots, (m + 1) * dm.slots)
-        stack_heads(turned[here, : dm.heads], b.QS.at[m])
+        stack_heads(turned[here, : dm.heads], lambda h: b.QS.at[m, h * dm.slots : (h + 1) * dm.slots])
         grid = (dm.slots, dm.slots)
         start_row = iota((dm.slots, 1), 0) - b.posc[here]
         start_col = iota((1, dm.slots), 1) - b.posr[m : m + 1]
@@ -326,46 +343,45 @@
             prob = expo / jnp.sum(expo, axis=-1, keepdims=True)
             prob = prob.reshape(span, dm.slots)
             b.PF[m, rows] = prob
-            b.DMS[rows] = mm(prob.astype(BF16), b.vd[kv, here]).astype(BF16)
+            dms[kv][...] = mm(prob.astype(BF16), b.vd[kv, here]).astype(BF16)
         for t in range(HEADS // 2):
-            even = b.DMS[2 * t * dm.slots : (2 * t + 1) * dm.slots]
-            odd = b.DMS[(2 * t + 1) * dm.slots : (2 * t + 2) * dm.slots]
-            b.mix[here, t * LANES : (t + 1) * LANES] = jnp.where(low, even, odd)
-    b.mpad[...] = mm(b.mix[...], b.spr[...]).astype(BF16)
+            even, odd = head_rows(2 * t)[...], head_rows(2 * t + 1)[...]
+            mix[here, t * LANES : (t + 1) * LANES] = jnp.where(low, even, odd)
+    b.mpad[...] = mm(mix[...], b.spr[...]).astype(BF16)
     hidden = xf + mm(b.mpad[...], W[:, dm.qkv :])
     b.hid[...] = hidden
     scale2 = lax.rsqrt(jnp.mean(hidden * hidden, axis=-1, keepdims=True) + 1e-06)
     nf = (hidden * scale2 * gain2).astype(BF16)
-    b.nfA[p] = mm(nf, b.spr[...]).astype(BF16)
+    b.nfA[p] = nf
 
     for k in range(1, CHIPS):
         send(b.nfA.at[p], b.nfA.at[p], b.rNF.at[p], dev(r, ((q + k) % CHIPS) * 2 + c))
     send(b.nfA.at[p], b.nfA.at[p], b.rNF.at[p], (partner,))
+    relay_gate(1)
     for k in range(1, CHIPS):
         place = ((q + CHIPS - k) % CHIPS) * 2 + c
         arrived(b.gA.at[place], b.rG.at[place])
         send(b.gA.at[place], b.gA.at[place], b.rG.at[place], (partner,))
+    for k in range(2, planes):
+        if k > 2:
+            relay_down(k)
+        relay_gate(k)
     for k in range(1, CHIPS):
         place = ((q + CHIPS - k) % CHIPS) * 2 + c
         arrived(b.nfA.at[place], b.rNF.at[place])
         send(b.nfA.at[place], b.nfA.at[place], b.rNF.at[place], (partner,))
-    for k in range(1, planes):
-        origin = (r + planes - k) % planes
-        arrived(plane_rows(b.GU, origin), b.rGZ.at[origin])
-    for slot in range(planes):
-        arrived(b.WD.at[slot], b.rWD.at[slot])
     keep[2].wait()
+    keep[3].wait()
     for k in range(CHIPS):
         place = ((q + CHIPS - k) % CHIPS) * 2 + other
         arrived(b.gA.at[place], b.rG.at[place])
         arrived(b.nfA.at[place], b.rNF.at[place])
 
-    GU = b.GU.reshape(dm.dp, 2 * dm.ffr)
+    ACT = b.act.reshape(PLANE * tok, dm.ffr)
     WD = b.WD.reshape(dm.ffr, dm.d)
-    BIG = b.BIG.reshape(dm.dp, 4 * dm.ffr)
     half = PLANE // 2
 
-    def feed(place_q, place_c, slot):
+    def feed(place_q, place_c):
         place = place_q * 2 + place_c
         nf_t, g_t = b.nfA[place], b.gA[place]
         pre = mm(nf_t, GU[...])
@@ -373,7 +389,7 @@
         sigma = jax.nn.sigmoid(gate)
         silu = gate * sigma
         act = (silu * upper).astype(BF16)
-        b.act[pl.ds(pl.multiple_of(place * tok, tok), tok), :] = act
+        ACT[pl.ds(pl.multiple_of(place * tok, tok), tok), :] = act
         b.oP[place_q, place_c] = mm(act, WD[...]).astype(BF16)
         d_act = mm_nt(g_t, WD[...])
         d_gate = (d_act * upper * (sigma + silu * (1.0 - sigma))).astype(BF16)
@@ -394,91 +410,118 @@
             device_id_type=MESH,
         )
 
+    def second_copy(k, part, landing, sems, arrive):
+        where = (q + k) % CHIPS
+        return pltpu.make_async_remote_copy(
+            src_ref=part.at[where, c],
+            dst_ref=landing.at[k - 1],
+            send_sem=sems.at[k - 1],
+            recv_sem=arrive.at[k - 1],
+            device_id=dev(r, where * 2 + c),
+            device_id_type=MESH,
+        )
+
+    def join(where):
+        for part, one, arrive in ((b.dP, b.dR1, b.rD1), (b.oP, b.oR1, b.rO1)):
+            arrived(one.at[where], arrive.at[where])
+            part[where, c] = (part[where, c].astype(F32) + one[where].astype(F32)).astype(BF16)
+
     @pl.loop(0, CHIPS)
     def _(step):
-        where = (q + step) % CHIPS
+        where = (q + 1 + step) % CHIPS
 
         @pl.loop(0, 2)
         def _(turn):
-            feed(where, (other + turn) % 2, step)
+            feed(where, (other + turn) % 2)
 
             @pl.when(turn == 0)
             def _():
+                first_copy(where, b.dP, b.dR1, b.dsem, b.rD1).start()
                 first_copy(where, b.oP, b.oR1, b.osem, b.rO1).start()
-                first_copy(where, b.dP, b.dR1, b.dsem, b.rD1).start()
-
-    for k in (1, 2, 3, 0):
-        where = (q + k) % CHIPS
-        arrived(b.oR1.at[where], b.rO1.at[where])
-        b.oP[where, c] = (b.oP[where, c].astype(F32) + b.oR1[where].astype(F32)).astype(BF16)
-        arrived(b.dR1.at[where], b.rD1.at[where])
-        b.dP[where, c] = (b.dP[where, c].astype(F32) + b.dR1[where].astype(F32)).astype(BF16)
-        if k:
-            send(b.dP.at[where, c], b.dR2.at[k - 1], b.rD2.at[k - 1], dev(r, where * 2 + c))
-            send(b.oP.at[where, c], b.oR2.at[k - 1], b.rO2.at[k - 1], dev(r, where * 2 + c))
-
-    for shift in range(planes):
-        origin, rank, slot, src = down_route(shift)
-
-        @pl.when(rank != p)
+
+        @pl.when(step > 0)
         def _():
-            down_copy(shift).wait_send()
+            join((q + step) % CHIPS)
+            second_copy(step, b.dP, b.dR2, b.dsem2, b.rD2).start()
+            second_copy(step, b.oP, b.oR2, b.osem2, b.rO2).start()
 
     drain()
-    nf_all = b.nfA.reshape(PLANE * tok, dm.dp)
+    join(q)
+
+    nf_all = b.nfA.reshape(PLANE * tok, dm.d)
     g_all = b.gA.reshape(PLANE * tok, dm.d)
-    wide_rows = dm.dp
-    chunk = dm.dp // 4
-
-    @pl.loop(0, 4)
-    def _(i):
-        cols = pl.ds(pl.multiple_of(i * chunk, chunk), chunk)
+    wide_rows = half * tok
+    chunk = 2 * LANES
+
+    def hop(part, landing, arrive, to, cond):
+        ahead = (to - r - 1 + planes) // planes
+        beyond = r - to - 1 + 2 * planes * ahead
+        last = 1 - (beyond + 4 * planes - 1) // (4 * planes)
+        slot = to + (planes - to) * last
+        send(part(to), landing.at[slot], arrive.at[slot], dev(r - 1 + 2 * ahead, p), cond)
+
+    def behind_of(to):
+        ahead = (to - r - 1 + planes) // planes
+        follows = r + 1 - 2 * ahead
+        return (follows >= 0) & (follows < planes)
+
+    far = [origin_of(planes - k) for k in range(1, planes)]
+
+    def chain_start(part, landing, arrive):
+        for to in far:
+            hop(part, landing, arrive, to, jnp.logical_not(behind_of(to)))
+
+    def chain_step(part, landing, arrive, k):
+        to = far[k]
+        has = behind_of(to)
+
+        @pl.when(has)
+        def _():
+            arrived(landing.at[to], arrive.at[to])
+            mine = part(to)
+            mine[...] = (mine[...].astype(F32) + landing[to].astype(F32)).astype(BF16)
+
+        hop(part, landing, arrive, to, has)
+
+    def chain_end(total, landing, arrive):
+        for slot, cond in ((r, r >= 1), (planes, r + 1 < planes)):
+
+            @pl.when(cond)
+            def _():
+                arrived(landing.at[slot], arrive.at[slot])
+                total[...] = (total[...].astype(F32) + landing[slot].astype(F32)).astype(total.dtype)
+
+    def gate_part(plane):
+        return plane_rows(b.GU, plane)
+
+    def down_part(plane):
+        return b.WD.at[plane]
+
+    def attn_part(plane):
+        return b.aR2.at[0, plane]
+
+    WD[...] = mm_tn(ACT[...], g_all[...]).astype(BF16)
+    chain_start(down_part, b.zD, b.rW)
+
+    def gate_grad(start, width):
+        cols = pl.ds(start, width)
         total = mm_tn(nf_all[:wide_rows, cols], BIG[:, : 2 * dm.ffr])
         total = total + mm_tn(nf_all[wide_rows:, cols], BIG[:, 2 * dm.ffr :])
         GU[cols, :] = total.astype(BF16)
 
-    for k in range(1, planes):
-        to = (r + k) % planes
-        send(plane_rows(b.GU, to), b.zR.at[k - 1], b.rZ.at[k - 1], dev(to, p))
-    WD[...] = mm_tn(b.act[...], g_all[...]).astype(BF16)
-
-    def down_back(slot):
-        whole = p * planes + slot
-        return whole // PLANE, whole % PLANE
-
-    def down_back_copy(slot):
-        plane_to, place_to = down_back(slot)
-        return pltpu.make_async_remote_copy(
-            src_ref=b.WD.at[slot],
-            dst_ref=b.dWDz.at[plane_to],
-            send_sem=b.vsem.at[slot],
-            recv_sem=b.rW1.at[plane_to],
-            device_id=dev(r, place_to),
-            device_id_type=MESH,
-        )
-
-    for slot in range(planes):
-        plane_to, place_to = down_back(slot)
-
-        @pl.when(place_to == p)
-        def _():
-            pltpu.make_async_copy(b.WD.at[slot], b.dWDz.at[plane_to], b.rW1.at[plane_to]).start()
-
-        @pl.when(place_to != p)
-        def _():
-            down_back_copy(slot).start()
-
+    @pl.loop(0, dm.d // chunk)
+    def _(i):
+        gate_grad(pl.multiple_of(i * chunk, chunk), chunk)
+
+    if dm.d % chunk:
+        gate_grad(dm.d - dm.d % chunk, dm.d % chunk)
+
+    chain_start(gate_part, b.zR, b.rZ)
     d_nf = b.dP[q, c].astype(F32)
-    total = b.oP[q, c].astype(F32)
     for k in range(1, CHIPS):
         arrived(b.dR2.at[k - 1], b.rD2.at[k - 1])
         d_nf = d_nf + b.dR2[k - 1].astype(F32)
-    for k in range(1, CHIPS):
-        arrived(b.oR2.at[k - 1], b.rO2.at[k - 1])
-        total = total + b.oR2[k - 1].astype(F32)
     hidden = b.hid[...]
-    b.out[...] = (hidden + total).astype(BF16)
-    d_nf = split_mm(d_nf, b.spr[...], nt=True)
     scale2 = lax.rsqrt(jnp.mean(hidden * hidden, axis=-1, keepdims=True) + 1e-06)
 
     def norm_back(grad, field, scale, gain):
@@ -491,26 +534,21 @@
 
     d_gain2, d_part = norm_back(d_nf, hidden, scale2, b.vec[2:3])
     d_hidden = b.g[...].astype(F32) + d_part
-    b.hid[...] = d_hidden
+    b.dhid[...] = d_hidden
     d_attn = d_hidden.astype(BF16)
-    for k in range(1, planes):
-        to = (r + k) % planes
-        arrived(b.dWDz.at[to], b.rW1.at[to])
-        send(b.dWDz.at[to], b.dWDr.at[k - 1], b.rW2.at[k - 1], dev(to, p))
-
     BIG[:, dm.qkv : dm.wide] = mm_tn(b.mpad[...], d_attn).astype(BF16)
     d_mixed = mm_nt(d_attn, W[:, dm.qkv :]).astype(BF16)
     d_mixed = mm_nt(d_mixed, b.spr[...])
     d_values = []
     for m in range(dm.micro):
         here = slice(m * dm.slots, (m + 1) * dm.slots)
-        stack_heads(d_mixed[here], b.DMS)
+        stack_heads(d_mixed[here], head_rows)
         d_v, d_k = [], []
         for kv in range(KV_HEADS):
             rows = slice(kv * span, (kv + 1) * span)
-            dms, prob, qs = b.DMS[rows], b.PF[m, rows], b.QS[m, rows]
-            d_v.append(mm_tn(prob.astype(BF16), dms))
-            d_prob = mm_nt(dms, b.vd[kv, here])
+            d_mix, prob, qs = dms[kv][...], b.PF[m, rows], b.QS[m, rows]
+            d_v.append(mm_tn(prob.astype(BF16), d_mix))
+            d_prob = mm_nt(d_mix, b.vd[kv, here])
             delta = jnp.sum(d_prob * prob, axis=-1, keepdims=True)
             d_score = (prob * (d_prob - delta)).astype(BF16)
             d_k.append(0.125 * mm_tn(d_score, qs))
@@ -538,7 +576,7 @@
     xf = b.x[...].astype(F32)
     scale1 = lax.rsqrt(jnp.mean(xf * xf, axis=-1, keepdims=True) + 1e-06)
     d_gain1, d_part = norm_back(d_normed, xf, scale1, b.vec[0:1])
-    b.gin[...] = (b.hid[...] + d_part).astype(BF16)
+    b.gin[...] = (b.dhid[...] + d_part).astype(BF16)
 
     rows8 = iota((8, dm.d), 0)
     packed = jnp.zeros((8, dm.d), F32)
@@ -563,11 +601,9 @@
     def quad(plane):
         return pl.ds(plane * CHIPS, CHIPS)
 
-    for k in (*range(1, planes), 0):
-        to = (r + k) % planes
+    for to in (*far, r):
         send(b.BIG.at[quad(to), other, :, cols], b.aR1.at[quad(to)], b.rA1.at[to], (partner,))
-    for k in (*range(1, planes), 0):
-        to = (r + k) % planes
+    for to in (*far, r):
         arrived(b.aR1.at[quad(to)], b.rA1.at[to])
         mine_now = b.BIG[quad(to), c, :, cols].astype(F32) + b.aR1[quad(to)].astype(F32)
         b.aR1[quad(to)] = mine_now.astype(BF16)
@@ -579,48 +615,49 @@
                 b.rA2.at[j - 1, to],
                 dev(r, where * 2 + c),
             )
-    mine_gu = plane_rows(b.GU, r)
-    total = mine_gu[...].astype(F32)
-    for k in range(1, planes):
-        arrived(b.zR.at[k - 1], b.rZ.at[k - 1])
-        total = total + b.zR[k - 1].astype(F32)
-    mine_gu[...] = total.astype(BF16)
-    for k in range(1, PLANE):
-        to = (p + k) % PLANE
-        send(b.GU.at[r * PLANE + to], b.fgu.at[p], b.rF.at[p], dev(r, to))
-    b.fgu[p] = b.GU[me]
-    for k in (*range(1, planes), 0):
-        to = (r + k) % planes
+    total = b.hid[...] + b.oP[q, c].astype(F32)
+    for k in range(1, CHIPS):
+        arrived(b.oR2.at[k - 1], b.rO2.at[k - 1])
+        total = total + b.oR2[k - 1].astype(F32)
+    b.out[...] = total.astype(BF16)
+    for k in range(planes - 1):
+        chain_step(down_part, b.zD, b.rW, k)
+    for k in range(planes - 2):
+        chain_step(gate_part, b.zR, b.rZ, k)
+    for to in (*far, r):
         total = b.aR1[to * CHIPS + q].astype(F32)
         for j in range(1, CHIPS):
             arrived(b.aR2.at[j - 1, to], b.rA2.at[j - 1, to])
             total = total + b.aR2[j - 1, to].astype(F32)
-        if k:
-            b.aR2[0, to] = total.astype(BF16)
-            send(b.aR2.at[0, to], b.aR3.at[k - 1], b.rA3.at[k - 1], dev(to, p))
-    arrived(b.dWDz.at[r], b.rW1.at[r])
-    down = b.dWDz[r].astype(F32)
-    for k in range(1, planes):
-        arrived(b.dWDr.at[k - 1], b.rW2.at[k - 1])
-        down = down + b.dWDr[k - 1].astype(F32)
-    b.fwd[...] = down
-    for k in range(1, planes):
-        arrived(b.aR3.at[k - 1], b.rA3.at[k - 1])
-        total = total + b.aR3[k - 1].astype(F32)
-    b.fa[...] = total
+        b.aR2[0, to] = total.astype(BF16)
+    chain_start(attn_part, b.aR3, b.rA3)
+    chain_step(gate_part, b.zR, b.rZ, planes - 2)
+    chain_end(gate_part(r), b.zR, b.rZ)
+    squeeze = b.spr[: dm.unit, : PLANE * rp]
+    for i in range(2):
+        piece = mm_tn(squeeze, GU[my_rows, i * dm.ffr : (i + 1) * dm.ffr]).astype(BF16)
+        piece = piece.reshape(PLANE, rp, dm.ffr)
+        for place in range(PLANE):
+            b.act[2 * place + i] = piece[place]
+    for k in range(1, PLANE):
+        to = (p + k) % PLANE
+        send(b.act.at[pl.ds(2 * to, 2)], b.fgu.at[p], b.rF.at[p], dev(r, to))
+    b.fgu[p] = b.act[pl.ds(2 * p, 2)]
+    for k in range(planes - 1):
+        chain_step(attn_part, b.aR3, b.rA3, k)
+    b.fwd[...] = b.WD[r].astype(F32)
+    chain_end(b.fwd, b.zD, b.rW)
+    b.fa[...] = b.aR2[0, r].astype(F32)
+    chain_end(b.fa, b.aR3, b.rA3)
     for k in range(1, PLANE):
         origin = (p + PLANE - k) % PLANE
         arrived(b.fgu.at[origin], b.rF.at[origin])
-    for slot in range(planes):
-        plane_to, place_to = down_back(slot)
-
-        @pl.when(place_to != p)
-        def _():
-            down_back_copy(slot).wait_send()
-
     for where in range(CHIPS):
         first_copy(where, b.oP, b.oR1, b.osem, b.rO1).wait_send()
         first_copy(where, b.dP, b.dR1, b.dsem, b.rD1).wait_send()
+    for k in range(1, CHIPS):
+        second_copy(k, b.oP, b.oR2, b.osem2, b.rO2).wait_send()
+        second_copy(k, b.dP, b.dR2, b.dsem2, b.rD2).wait_send()
     drain()
 
 
@@ -634,68 +671,63 @@
         "out": jax.ShapeDtypeStruct((tok, dm.d), BF16),
         "gin": jax.ShapeDtypeStruct((tok, dm.d), BF16),
         "fa": jax.ShapeDtypeStruct((rp, dm.wide), F32),
-        "fgu": jax.ShapeDtypeStruct((PLANE, rp, 2 * dm.ffr), BF16),
+        "fgu": jax.ShapeDtypeStruct((PLANE, 2, rp, dm.ffr), BF16),
         "fwd": jax.ShapeDtypeStruct((dm.rfp, dm.d), F32),
     }
     n_sends = 1 + (planes - 1) * 5 + 8 * PLANE + 8 * quads + 64
     scratch = {
         "W": vm((quads, 2, rp, dm.wide), BF16),
-        "GU": vm((n, rp, 2 * dm.ffr), BF16),
-        "WDz": vm((planes, dm.rfp, dm.d), BF16),
+        "GU": vm((planes * dm.groups, dm.gs, 2 * dm.ffr), BF16),
         "WD": vm((planes, dm.rfp, dm.d), BF16),
-        "nfA": vm((PLANE, tok, dm.dp), BF16),
+        "nfA": vm((PLANE, tok, dm.d), BF16),
         "gA": vm((PLANE, tok, dm.d), BF16),
-        "act": vm((PLANE * tok, dm.ffr), BF16),
+        "act": vm((PLANE * tok // rp, rp, dm.ffr), BF16),
         "BIG": vm((quads, 2, rp, 4 * dm.ffr), BF16),
         "oP": vm((CHIPS, 2, tok, dm.d), BF16),
-        "dP": vm((CHIPS, 2, tok, dm.dp), BF16),
+        "dP": vm((CHIPS, 2, tok, dm.d), BF16),
         "oR1": vm((CHIPS, tok, dm.d), BF16),
-        "dR1": vm((CHIPS, tok, dm.dp), BF16),
+        "dR1": vm((CHIPS, tok, dm.d), BF16),
         "oR2": vm((CHIPS - 1, tok, dm.d), BF16),
-        "dR2": vm((CHIPS - 1, tok, dm.dp), BF16),
-        "zR": vm((planes - 1, PLANE, rp, 2 * dm.ffr), BF16),
-        "dWDz": vm((planes, dm.rfp, dm.d), BF16),
-        "dWDr": vm((planes - 1, dm.rfp, dm.d), BF16),
+        "dR2": vm((CHIPS - 1, tok, dm.d), BF16),
+        "zR": vm((planes + 1, dm.groups, dm.gs, 2 * dm.ffr), BF16),
+        "zD": vm((planes + 1, dm.rfp, dm.d), BF16),
         "aR1": vm((quads, rp, dm.wide), BF16),
         "aR2": vm((CHIPS - 1, planes, rp, dm.wide), BF16),
-        "aR3": vm((planes - 1, rp, dm.wide), BF16),
+        "aR3": vm((planes + 1, rp, dm.wide), BF16),
         "QS": vm((dm.micro, HEADS * dm.slots, LANES), BF16),
         "PF": vm((dm.micro, HEADS * dm.slots, dm.slots), F32),
-        "DMS": vm((HEADS * dm.slots, LANES), BF16),
         "hid": vm((tok, dm.d), F32),
+        "dhid": vm((tok, dm.d), F32),
         "npad": vm((tok, dm.dp), BF16),
         "mpad": vm((tok, dm.dp), BF16),
         "spr": vm((dm.d, dm.dp), BF16),
         "kd": vm((KV_HEADS, tok, LANES), BF16),
         "vd": vm((KV_HEADS, tok, LANES), BF16),
         "FQ": vm((tok, pairs), F32),
-        "mix": vm((tok, dm.d), BF16),
         "tabs": vm((2, tok, LANES), F32),
         "vec": vm((8, dm.d), F32),
         "ssem": sem((n_sends,)),
-        "csem": sem((3,)),
+        "csem": sem((4,)),
         "osem": sem((CHIPS,)),
         "dsem": sem((CHIPS,)),
-        "wsem": sem((planes,)),
-        "vsem": sem((planes,)),
+        "osem2": sem((CHIPS - 1,)),
+        "dsem2": sem((CHIPS - 1,)),
         "rA": sem((n,)),
         "rGU": sem((PLANE,)),
         "rGZ": sem((planes,)),
         "rG": sem((PLANE,)),
-        "rWZ": sem((planes,)),
         "rWD": sem((planes,)),
         "rNF": sem((PLANE,)),
         "rO1": sem((CHIPS,)),
         "rD1": sem((CHIPS,)),
         "rO2": sem((CHIPS - 1,)),
         "rD2": sem((CHIPS - 1,)),
-        "rZ": sem((planes - 1,)),
+        "rZ": sem((planes + 1,)),
         "rF": sem((PLANE,)),
-        "rW1": sem((planes,)),
-        "rW2": sem((planes - 1,)),
+        "rW": sem((planes + 1,)),
         "rA1": sem((planes,)),
         "rA2": sem((CHIPS - 1, planes)),
-        "rA3": sem((planes - 1,)),
+        "rA3": sem((planes + 1,)),
     }
     return pl.pallas_call(
         functools.partial(layer_kernel, dm, (*operands, *outs, *scratch)),
@@ -744,12 +776,11 @@
     pack = jnp.pad(pack, ((0, rp - rows - 1), (0, 0)))
 
     def columns(weight):
-        weight = weight.reshape(rows, PLANE, dm.planes, dm.rf)
+        weight = weight.reshape(rows, dm.planes, PLANE, dm.rf)
         weight = jnp.pad(weight, ((0, rp - rows), (0, 0), (0, 0), (0, dm.rfp - dm.rf)))
-        return weight.reshape(rp, PLANE, dm.ffr)
-
-    both = jnp.concatenate([columns(w_gate), columns(w_up)], axis=2)
-    both = both.transpose(1, 0, 2)
+        return weight.transpose(2, 0, 1, 3).reshape(PLANE, rp, dm.ffr)
+
+    both = jnp.stack([columns(w_gate), columns(w_up)], axis=1)
     down = jnp.pad(w_down.reshape(dm.rf, d), ((0, dm.rfp - dm.rf), (0, 0)))
     half_dim = HEAD_DIM // 2
     freq = 1000000.0 ** (-(jnp.arange(half_dim).astype(F32) * 2.0 / HEAD_DIM))
@@ -773,10 +804,10 @@
     def flat(start, stop):
         return fa[:rows, start:stop].reshape(-1)
 
-    def gate_part(start):
-        part = fgu[:, :rows, start : start + dm.ffr].astype(F32)
+    def gate_part(i):
+        part = fgu[:, i, :rows].astype(F32)
         part = part.reshape(PLANE, rows, dm.planes, dm.rfp)[..., : dm.rf]
-        return part.transpose(1, 0, 2, 3).reshape(-1)
+        return part.transpose(1, 2, 0, 3).reshape(-1)
 
     h, kv = dm.heads, dm.kv
     return (
@@ -792,7 +823,7 @@
         flat(h + 2 * kv, dm.wide),
         field(2, rows),
         gate_part(0),
-        gate_part(dm.ffr),
+        gate_part(1),
         fwd[: dm.rf].reshape(-1),
     )
 

time: 308 us -> 223 us (0.72)
  the two profiles are of different devices: /device:TPU:28 before, /device:TPU:0 now
where the time goes in v2:
time: 223 us; the launch traced here: 222 us
  Pallas kernels  195 us (87%)
  local copies, waits for them, and re-layouts  24.3 us (11%)
    pallas_call x1, Pallas kernels, run_layer(): pl.pallas_call(functools.partial(layer_kernel, dm, (*operands, *outs, *sc...  195 us

profile of v2, /device:TPU:0, one launch (start us, length us, event | category | flops | bytes accessed | tf_op | source)
XLA Modules:
  0.0 222.2 jit_solution(2613582305178181889)
XLA Ops:
  0.7 0.6 copy-done.14
  1.4 0.6 broadcast_in_dim_tile.3.refs_4_
  2.1 0.9 reshape.109
  3.1 0.7 fusion.8.refs_6_
  3.8 0.8 copy.31.refs_2_
  4.9 0.7 pad.41.refs_8_
  6.0 1.3 reshape.113
  7.9 0.6 copy-done.6
  8.6 1.3 reshape.114
  10.5 0.9 pad_maximum_fusion.refs_7_
  11.5 195.0 %layer.1 = (bf16[256,896]{1,0:T(8,128)(2,1)}, bf16[256,896]{1,0:T(8,128)(2,1)}, f32[32,2048]{1,0:T(8,128)}, bf16[8,2,32,640]{3,2,1,0:T(8,128)(2,1)}, f32[160,896]{1,0:T(8,128)}) custom-call(bf16[256,896]{1,0:T(8,128)(2,1)} %bitcast.42, bf16[256,896]{1,0:T(8,128)(2,1)} %bitcast.43, s32[256,1]{1,0:T(8,128)} %copy.31.refs_2_, s32[2,128]{1,0:T(2,128)} %refs_3_.1, ...), custom_call_target="tpu_custom_call" | custom-call | tf_op jit(solution)/shard_map/layer/pallas_call | solution.py:732
  206.5 1.2 slice_bitcast_fusion.4
  207.7 1.3 slice_bitcast_fusion.3
  209.0 1.4 slice_bitcast_fusion.2
  210.4 1.3 slice_bitcast_fusion
  211.7 1.0 fusion.13
  212.7 0.7 reshape.121
  213.3 0.7 reshape.118
  214.0 0.8 reshape.126
  214.9 0.4 copy-done
  216.5 1.7 reshape.128
  218.5 1.7 reshape.130
  220.2 0.8 copy.38
  221.4 0.8 copy.39
  (50 shorter events, 4.0 us)
Async XLA Ops:
  0.6 0.7 copy-start.14
  0.7 0.7 copy-start.11
  0.7 0.7 copy-start.12
  0.7 0.7 copy-start.13
  2.1 0.9 copy-start.7
  2.1 1.0 copy-start.8
  2.1 1.0 copy-start.9
  3.0 1.6 copy-start.4
  3.1 0.7 copy-start.10
  4.9 1.0 copy-start.5
  7.6 1.0 copy-start.6
  206.5 7.5 %copy-start.1 = (f32[160,896]{1,0:T(8,128)S(1)}, f32[160,896]{1,0:T(8,128)}, u32[]{:S(2)}) copy-start(f32[160,896]{1,0:T(8,128)} %get-tuple-element.23) | copy-start | bytes 1720324
  214.0 1.3 copy-start
  218.5 1.7 copy-start.3
  220.2 1.2 copy-start.2

commit v3 on v2

--- a/solution.py
+++ b/solution.py
@@ -1,4 +1,5 @@
 import functools
+import math
 
 import jax
 import jax.numpy as jnp
@@ -14,6 +15,7 @@
 PLANE = 8
 CHIPS = 4
 LANES = 128
+ROTARY_LOG = math.log(1000000.0)
 FIELD = 32
 MESH = pl.DeviceIdType.MESH
 F32 = jnp.float32
@@ -69,6 +71,9 @@
         self.unit = PLANE * self.rows
         self.gs = 16 if self.unit % 16 == 0 else 8
         self.groups = self.unit // self.gs
+        blocks = self.ffr // LANES
+        wide = (blocks + 1) // 2 * LANES
+        self.parts = ((0, wide), (wide, self.ffr - wide))
 
 
 def spread_matrix(dm):
@@ -149,7 +154,7 @@
     pending = []
     count = [0]
 
-    def send(src, dst, arrive, to, cond=None):
+    def prepare(src, dst, arrive, to, cond=None, tag=None):
         copy = pltpu.make_async_remote_copy(
             src_ref=src,
             dst_ref=dst,
@@ -159,19 +164,24 @@
             device_id_type=MESH,
         )
         count[0] += 1
-        pending.append((copy, cond))
+        pending.append((copy, cond, tag))
+        return copy
+
+    def send(src, dst, arrive, to, cond=None, tag=None):
+        copy = prepare(src, dst, arrive, to, cond, tag)
         if cond is None:
             copy.start()
         else:
             pl.when(cond)(copy.start)
 
-    def drain(left=0):
-        for copy, cond in pending[: len(pending) - left]:
+    def drain(tag=None):
+        now = [item for item in pending if tag in (None, item[2])]
+        for copy, cond, _ in now:
             if cond is None:
                 copy.wait_send()
             else:
                 pl.when(cond)(copy.wait_send)
-        del pending[: len(pending) - left]
+        pending[:] = [item for item in pending if tag not in (None, item[2])]
 
     upper = r // max(planes // 2, 1)
     mirror = r + upper * (planes - 1 - 2 * r)
@@ -180,13 +190,25 @@
         spot = k - (mirror + planes - k) // planes
         return spot + upper * (planes - 1 - 2 * spot)
 
-    def relay(src, dst, arrive, origin=None):
-        if origin is None:
-            send(src, dst, arrive, dev(r + 1, p), r + 1 < planes)
-            send(src, dst, arrive, dev(r - 1, p), r >= 1)
-        else:
-            to = r - 1 + 2 * ((r - origin - 1 + planes) // planes)
-            send(src, dst, arrive, dev(to, p), (to >= 0) & (to < planes))
+    def relay_own(src, dst, arrive, tag=None):
+        send(src, dst, arrive, dev(r + 1, p), r + 1 < planes, tag)
+        send(src, dst, arrive, dev(r - 1, p), r >= 1, tag)
+
+    def onward(part, sems, k, tag=None):
+        origin = origin_of(k)
+        to = r - 1 + 2 * ((r - origin - 1 + planes) // planes)
+        cond = (to >= 0) & (to < planes)
+        piece, arrive = part(origin), sems.at[origin]
+        return piece, arrive, cond, prepare(piece, piece, arrive, dev(to, p), cond, tag)
+
+    def pass_on(piece, arrive, cond, copy):
+        @pl.when(cond)
+        def _():
+            arrived(piece, arrive)
+            copy.start()
+
+    def settle(piece, arrive, cond, copy):
+        pl.when(jnp.logical_not(cond))(lambda: arrived(piece, arrive))
 
     def arrived(dst, arrive):
         pltpu.make_async_remote_copy(
@@ -213,22 +235,46 @@
     for copy in keep:
         copy.start()
 
-    relay(b.ap, block(b.W, me), b.rA.at[me])
-
-    def fan(index, src, k_list=(1, 2, 3)):
-        for k in k_list:
-            send(src, block(b.W, index), b.rA.at[index], dev(r, ((q + k) % CHIPS) * 2 + c))
+    relay_own(b.ap, block(b.W, me), b.rA.at[me])
+
+    across, along = q + 1 - 2 * (q % 2), (q + 2) % CHIPS
+    near = across * other + along * c
+    next_to = along * other + across * c
+    spots = (near, next_to, CHIPS - 1 - q)
+
+    def fan(index, src):
+        for where in (next_to, near):
+            send(src, block(b.W, index), b.rA.at[index], dev(r, where * 2 + c))
+
+    def spread_out(src, ref, arrive):
+        for where in (next_to, near):
+            send(src, ref.at[p], arrive.at[p], dev(r, where * 2 + c))
+        send(src, ref.at[p], arrive.at[p], (partner,))
+
+    def take_in(ref, arrive):
+        for i, where in enumerate(spots):
+            place = where * 2 + c
+            arrived(ref.at[place], arrive.at[place])
+            if i == 0:
+                send(ref.at[place], ref.at[place], arrive.at[place], dev(r, next_to * 2 + c))
+            send(ref.at[place], ref.at[place], arrive.at[place], (partner,))
 
     fan(me, b.ap)
     send(b.ap, block(b.W, me), b.rA.at[me], (partner,))
     for k in range(1, PLANE):
         send(b.gus.at[(p + k) % PLANE], b.fgu.at[p], b.rGU.at[p], dev(r, (p + k) % PLANE))
-    relay(b.wds, b.WD.at[r], b.rWD.at[r])
+    relay_own(b.wds, b.WD.at[r], b.rWD.at[r])
 
     tok = dm.tok
     xf = b.x[...].astype(F32)
     scale1 = lax.rsqrt(jnp.mean(xf * xf, axis=-1, keepdims=True) + 1e-06)
-    angle = b.posc[...].astype(F32) * b.freq[...]
+    diagonal = iota((dm.slots, dm.slots), 0) == iota((dm.slots, dm.slots), 1)
+    posc = [
+        jnp.sum(jnp.where(diagonal, b.posr[m : m + 1].astype(F32), 0.0), axis=1, keepdims=True)
+        for m in range(dm.micro)
+    ]
+    power = (iota((1, LANES), 1) & (HEAD_DIM // 2 - 1)).astype(F32) * (-2.0 / HEAD_DIM * ROTARY_LOG)
+    angle = jnp.concatenate(posc, axis=0) * jnp.exp(power)
     b.tabs[0] = jnp.cos(angle)
     b.tabs[1] = jnp.sin(angle)
     b.spr[...] = spread_matrix(dm)
@@ -237,43 +283,45 @@
         origin = origin_of(k)
         index = origin * PLANE + p
         arrived(block(b.W, index), b.rA.at[index])
-        relay(block(b.W, index), block(b.W, index), b.rA.at[index], origin)
+        to = r - 1 + 2 * ((r - origin - 1 + planes) // planes)
+        send(block(b.W, index), block(b.W, index), b.rA.at[index], dev(to, p), (to >= 0) & (to < planes))
         fan(index, block(b.W, index))
         send(block(b.W, index), block(b.W, index), b.rA.at[index], (partner,))
     for k in range(1, PLANE):
         origin = (p + PLANE - k) % PLANE
         arrived(b.fgu.at[origin], b.rGU.at[origin])
     keep[1].wait()
-    GU = b.GU.reshape(dm.d, 2 * dm.ffr)
+    GU = [ref.reshape(dm.d, ref.shape[-1]) for ref in (b.GU0, b.GU1)]
     my_rows = pl.ds(pl.multiple_of(r * dm.unit, dm.gs), dm.unit)
     squeeze = b.spr[: dm.unit, : PLANE * rp]
-    for i in range(2):
-        piece = b.fgu[:, i].reshape(PLANE * rp, dm.ffr)
-        GU[my_rows, i * dm.ffr : (i + 1) * dm.ffr] = mm(squeeze, piece).astype(BF16)
-    relay(plane_rows(b.GU, r), plane_rows(b.GU, r), b.rGZ.at[r])
-
-    def relay_down(k):
-        origin = origin_of(k)
-        arrived(b.WD.at[origin], b.rWD.at[origin])
-        relay(b.WD.at[origin], b.WD.at[origin], b.rWD.at[origin], origin)
-
-    def relay_gate(k):
-        origin = origin_of(k)
-        arrived(plane_rows(b.GU, origin), b.rGZ.at[origin])
-        relay(plane_rows(b.GU, origin), plane_rows(b.GU, origin), b.rGZ.at[origin], origin)
-
-    relay_down(1)
-    for k in range(1, CHIPS):
-        for shift in range(planes):
-            index = ((r + planes - shift) % planes) * PLANE + ((q + CHIPS - k) % CHIPS) * 2 + c
+    for h, (start, width) in enumerate(dm.parts):
+        for i in range(2):
+            piece = b.fgu[:, i, :, start : start + width].reshape(PLANE * rp, width)
+            GU[h][my_rows, i * width : (i + 1) * width] = mm(squeeze, piece).astype(BF16)
+
+    def gate_part(h):
+        ref = (b.GU0, b.GU1)[h]
+        return lambda plane: plane_rows(ref, plane)
+
+    def down_part(plane):
+        return b.WD.at[plane]
+
+    relay_own(gate_part(0)(r), gate_part(0)(r), b.rGZ0.at[r], "gate0")
+    steps = range(1, planes)
+    down_on = [onward(down_part, b.rWD, k, "down") for k in steps]
+    gate_on = [[onward(gate_part(h), sems, k, f"gate{h}") for k in steps] for h, sems in ((0, b.rGZ0), (1, b.rGZ1))]
+    pass_on(*down_on[0])
+    origins = [r, *(origin_of(k) for k in steps)]
+    for i, where in enumerate(spots):
+        for origin in origins:
+            index = origin * PLANE + where * 2 + c
             arrived(block(b.W, index), b.rA.at[index])
+            if i == 0:
+                send(block(b.W, index), block(b.W, index), b.rA.at[index], dev(r, next_to * 2 + c))
             send(block(b.W, index), block(b.W, index), b.rA.at[index], (partner,))
-    for k in range(1, CHIPS):
-        send(b.g, b.gA.at[p], b.rG.at[p], dev(r, ((q + k) % CHIPS) * 2 + c))
-    send(b.g, b.gA.at[p], b.rG.at[p], (partner,))
-
-    for k in range(2, min(planes, 3)):
-        relay_down(k)
+    spread_out(b.g, b.gA, b.rG)
+    for item in down_on[1:]:
+        pass_on(*item)
 
     keep[0].wait()
     for k in range(CHIPS):
@@ -331,8 +379,8 @@
         here = slice(m * dm.slots, (m + 1) * dm.slots)
         stack_heads(turned[here, : dm.heads], lambda h: b.QS.at[m, h * dm.slots : (h + 1) * dm.slots])
         grid = (dm.slots, dm.slots)
-        start_row = iota((dm.slots, 1), 0) - b.posc[here]
-        start_col = iota((1, dm.slots), 1) - b.posr[m : m + 1]
+        start_row = iota((dm.slots, 1), 0).astype(F32) - posc[m]
+        start_col = (iota((1, dm.slots), 1) - b.posr[m : m + 1]).astype(F32)
         allowed = (start_row == start_col) & (iota(grid, 1) <= iota(grid, 0))
         for kv in range(KV_HEADS):
             rows = slice(kv * span, (kv + 1) * span)
@@ -354,22 +402,16 @@
     nf = (hidden * scale2 * gain2).astype(BF16)
     b.nfA[p] = nf
 
-    for k in range(1, CHIPS):
-        send(b.nfA.at[p], b.nfA.at[p], b.rNF.at[p], dev(r, ((q + k) % CHIPS) * 2 + c))
-    send(b.nfA.at[p], b.nfA.at[p], b.rNF.at[p], (partner,))
-    relay_gate(1)
-    for k in range(1, CHIPS):
-        place = ((q + CHIPS - k) % CHIPS) * 2 + c
-        arrived(b.gA.at[place], b.rG.at[place])
-        send(b.gA.at[place], b.gA.at[place], b.rG.at[place], (partner,))
-    for k in range(2, planes):
-        if k > 2:
-            relay_down(k)
-        relay_gate(k)
-    for k in range(1, CHIPS):
-        place = ((q + CHIPS - k) % CHIPS) * 2 + c
-        arrived(b.nfA.at[place], b.rNF.at[place])
-        send(b.nfA.at[place], b.nfA.at[place], b.rNF.at[place], (partner,))
+    spread_out(b.nfA.at[p], b.nfA, b.rNF)
+    pass_on(*gate_on[0][0])
+    relay_own(gate_part(1)(r), gate_part(1)(r), b.rGZ1.at[r], "gate1")
+    take_in(b.gA, b.rG)
+    for item in gate_on[0][1:]:
+        pass_on(*item)
+    take_in(b.nfA, b.rNF)
+    for item in (*down_on, *gate_on[0]):
+        settle(*item)
+    pass_on(*gate_on[1][0])
     keep[2].wait()
     keep[3].wait()
     for k in range(CHIPS):
@@ -381,24 +423,30 @@
     WD = b.WD.reshape(dm.ffr, dm.d)
     half = PLANE // 2
 
-    def feed(place_q, place_c):
+    base = (0, 4 * dm.parts[0][1])
+
+    def feed(h, place_q, place_c):
         place = place_q * 2 + place_c
+        start, width = dm.parts[h]
         nf_t, g_t = b.nfA[place], b.gA[place]
-        pre = mm(nf_t, GU[...])
-        gate, upper = pre[:, : dm.ffr], pre[:, dm.ffr :]
+        down = WD[start : start + width]
+        pre = mm(nf_t, GU[h][...])
+        gate, upper = pre[:, :width], pre[:, width:]
         sigma = jax.nn.sigmoid(gate)
         silu = gate * sigma
         act = (silu * upper).astype(BF16)
-        ACT[pl.ds(pl.multiple_of(place * tok, tok), tok), :] = act
-        b.oP[place_q, place_c] = mm(act, WD[...]).astype(BF16)
-        d_act = mm_nt(g_t, WD[...])
+        ACT[pl.ds(pl.multiple_of(place * tok, tok), tok), start : start + width] = act
+        d_act = mm_nt(g_t, down)
         d_gate = (d_act * upper * (sigma + silu * (1.0 - sigma))).astype(BF16)
         d_up = (d_act * silu).astype(BF16)
         d_both = jnp.concatenate([d_gate, d_up], axis=1)
         rows = pl.ds(pl.multiple_of((place % half) * tok, tok), tok)
-        cols = pl.ds(pl.multiple_of((place // half) * 2 * dm.ffr, LANES), 2 * dm.ffr)
+        cols = pl.ds(pl.multiple_of(base[h] + (place // half) * 2 * width, LANES), 2 * width)
         BIG[rows, cols] = d_both
-        b.dP[place_q, place_c] = mm_nt(d_both, GU[...]).astype(BF16)
+        for ref, value in ((b.oP, mm(act, down)), (b.dP, mm_nt(d_both, GU[h][...]))):
+            if h:
+                value = value + ref[place_q, place_c].astype(F32)
+            ref[place_q, place_c] = value.astype(BF16)
 
     def first_copy(where, part, landing, sems, arrive):
         return pltpu.make_async_remote_copy(
@@ -421,38 +469,6 @@
             device_id_type=MESH,
         )
 
-    def join(where):
-        for part, one, arrive in ((b.dP, b.dR1, b.rD1), (b.oP, b.oR1, b.rO1)):
-            arrived(one.at[where], arrive.at[where])
-            part[where, c] = (part[where, c].astype(F32) + one[where].astype(F32)).astype(BF16)
-
-    @pl.loop(0, CHIPS)
-    def _(step):
-        where = (q + 1 + step) % CHIPS
-
-        @pl.loop(0, 2)
-        def _(turn):
-            feed(where, (other + turn) % 2)
-
-            @pl.when(turn == 0)
-            def _():
-                first_copy(where, b.dP, b.dR1, b.dsem, b.rD1).start()
-                first_copy(where, b.oP, b.oR1, b.osem, b.rO1).start()
-
-        @pl.when(step > 0)
-        def _():
-            join((q + step) % CHIPS)
-            second_copy(step, b.dP, b.dR2, b.dsem2, b.rD2).start()
-            second_copy(step, b.oP, b.oR2, b.osem2, b.rO2).start()
-
-    drain()
-    join(q)
-
-    nf_all = b.nfA.reshape(PLANE * tok, dm.d)
-    g_all = b.gA.reshape(PLANE * tok, dm.d)
-    wide_rows = half * tok
-    chunk = 2 * LANES
-
     def hop(part, landing, arrive, to, cond):
         ahead = (to - r - 1 + planes) // planes
         beyond = r - to - 1 + 2 * planes * ahead
@@ -491,32 +507,79 @@
                 arrived(landing.at[slot], arrive.at[slot])
                 total[...] = (total[...].astype(F32) + landing[slot].astype(F32)).astype(total.dtype)
 
-    def gate_part(plane):
-        return plane_rows(b.GU, plane)
-
-    def down_part(plane):
-        return b.WD.at[plane]
+    nf_all = b.nfA.reshape(PLANE * tok, dm.d)
+    g_all = b.gA.reshape(PLANE * tok, dm.d)
+    wide_rows = half * tok
+    chunk = 2 * LANES
+
+    def gate_grad(h):
+        width = dm.parts[h][1]
+
+        def some(start, count):
+            cols = pl.ds(start, count)
+            total = mm_tn(nf_all[:wide_rows, cols], BIG[:, base[h] : base[h] + 2 * width])
+            total = total + mm_tn(nf_all[wide_rows:, cols], BIG[:, base[h] + 2 * width : base[h] + 4 * width])
+            GU[h][cols, :] = total.astype(BF16)
+
+        @pl.loop(0, dm.d // chunk)
+        def _(i):
+            some(pl.multiple_of(i * chunk, chunk), chunk)
+
+        if dm.d % chunk:
+            some(dm.d - dm.d % chunk, dm.d % chunk)
+
+    @pl.loop(0, PLANE)
+    def _(turn):
+        feed(0, turn // 2, turn % 2)
+
+        @pl.when(turn == half - 1)
+        def _():
+            for item in gate_on[1][1:]:
+                pass_on(*item)
+
+    drain("gate0")
+    gate_grad(0)
+    chain_start(gate_part(0), b.zR0, b.rZ0)
+    for item in gate_on[1]:
+        settle(*item)
+
+    def join(where):
+        for part, one, arrive in ((b.dP, b.dR1, b.rD1), (b.oP, b.oR1, b.rO1)):
+            arrived(one.at[where], arrive.at[where])
+            part[where, c] = (part[where, c].astype(F32) + one[where].astype(F32)).astype(BF16)
+
+    @pl.loop(0, CHIPS)
+    def _(step):
+        where = (q + 1 + step) % CHIPS
+
+        @pl.loop(0, 2)
+        def _(turn):
+            feed(1, where, (other + turn) % 2)
+
+            @pl.when(turn == 0)
+            def _():
+                first_copy(where, b.dP, b.dR1, b.dsem, b.rD1).start()
+                first_copy(where, b.oP, b.oR1, b.osem, b.rO1).start()
+
+        @pl.when(step > 0)
+        def _():
+            join((q + step) % CHIPS)
+            second_copy(step, b.dP, b.dR2, b.dsem2, b.rD2).start()
+
+    for k in range(1, CHIPS):
+        second_copy(k, b.oP, b.oR2, b.osem2, b.rO2).start()
+    join(q)
 
     def attn_part(plane):
         return b.aR2.at[0, plane]
 
+    drain("down")
     WD[...] = mm_tn(ACT[...], g_all[...]).astype(BF16)
     chain_start(down_part, b.zD, b.rW)
-
-    def gate_grad(start, width):
-        cols = pl.ds(start, width)
-        total = mm_tn(nf_all[:wide_rows, cols], BIG[:, : 2 * dm.ffr])
-        total = total + mm_tn(nf_all[wide_rows:, cols], BIG[:, 2 * dm.ffr :])
-        GU[cols, :] = total.astype(BF16)
-
-    @pl.loop(0, dm.d // chunk)
-    def _(i):
-        gate_grad(pl.multiple_of(i * chunk, chunk), chunk)
-
-    if dm.d % chunk:
-        gate_grad(dm.d - dm.d % chunk, dm.d % chunk)
-
-    chain_start(gate_part, b.zR, b.rZ)
+    drain("gate1")
+    gate_grad(1)
+    chain_start(gate_part(1), b.zR1, b.rZ1)
+    chain_step(gate_part(0), b.zR0, b.rZ0, 0)
     d_nf = b.dP[q, c].astype(F32)
     for k in range(1, CHIPS):
         arrived(b.dR2.at[k - 1], b.rD2.at[k - 1])
@@ -620,10 +683,12 @@
         arrived(b.oR2.at[k - 1], b.rO2.at[k - 1])
         total = total + b.oR2[k - 1].astype(F32)
     b.out[...] = total.astype(BF16)
+    for k in range(1, planes - 1):
+        chain_step(gate_part(0), b.zR0, b.rZ0, k)
     for k in range(planes - 1):
         chain_step(down_part, b.zD, b.rW, k)
     for k in range(planes - 2):
-        chain_step(gate_part, b.zR, b.rZ, k)
+        chain_step(gate_part(1), b.zR1, b.rZ1, k)
     for to in (*far, r):
         total = b.aR1[to * CHIPS + q].astype(F32)
         for j in range(1, CHIPS):
@@ -631,18 +696,25 @@
             total = total + b.aR2[j - 1, to].astype(F32)
         b.aR2[0, to] = total.astype(BF16)
     chain_start(attn_part, b.aR3, b.rA3)
-    chain_step(gate_part, b.zR, b.rZ, planes - 2)
-    chain_end(gate_part(r), b.zR, b.rZ)
     squeeze = b.spr[: dm.unit, : PLANE * rp]
-    for i in range(2):
-        piece = mm_tn(squeeze, GU[my_rows, i * dm.ffr : (i + 1) * dm.ffr]).astype(BF16)
-        piece = piece.reshape(PLANE, rp, dm.ffr)
-        for place in range(PLANE):
-            b.act[2 * place + i] = piece[place]
-    for k in range(1, PLANE):
-        to = (p + k) % PLANE
-        send(b.act.at[pl.ds(2 * to, 2)], b.fgu.at[p], b.rF.at[p], dev(r, to))
-    b.fgu[p] = b.act[pl.ds(2 * p, 2)]
+
+    def home(h, landing, arrive, final):
+        start, width = dm.parts[h]
+        cols = pl.ds(start, width)
+        chain_end(gate_part(h)(r), landing, arrive)
+        for i in range(2):
+            piece = mm_tn(squeeze, GU[h][my_rows, i * width : (i + 1) * width]).astype(BF16)
+            piece = piece.reshape(PLANE, rp, width)
+            for place in range(PLANE):
+                b.act[2 * place + i, :, cols] = piece[place]
+        for k in range(1, PLANE):
+            to = (p + k) % PLANE
+            send(b.act.at[pl.ds(2 * to, 2), :, cols], b.fgu.at[p, :, :, cols], final.at[p], dev(r, to))
+        b.fgu[p, :, :, cols] = b.act[pl.ds(2 * p, 2), :, cols]
+
+    home(0, b.zR0, b.rZ0, b.rF0)
+    chain_step(gate_part(1), b.zR1, b.rZ1, planes - 2)
+    home(1, b.zR1, b.rZ1, b.rF1)
     for k in range(planes - 1):
         chain_step(attn_part, b.aR3, b.rA3, k)
     b.fwd[...] = b.WD[r].astype(F32)
@@ -651,7 +723,8 @@
     chain_end(b.fa, b.aR3, b.rA3)
     for k in range(1, PLANE):
         origin = (p + PLANE - k) % PLANE
-        arrived(b.fgu.at[origin], b.rF.at[origin])
+        for (start, width), final in zip(dm.parts, (b.rF0, b.rF1)):
+            arrived(b.fgu.at[origin, :, :, pl.ds(start, width)], final.at[origin])
     for where in range(CHIPS):
         first_copy(where, b.oP, b.oR1, b.osem, b.rO1).wait_send()
         first_copy(where, b.dP, b.dR1, b.dsem, b.rD1).wait_send()
@@ -674,10 +747,11 @@
         "fgu": jax.ShapeDtypeStruct((PLANE, 2, rp, dm.ffr), BF16),
         "fwd": jax.ShapeDtypeStruct((dm.rfp, dm.d), F32),
     }
-    n_sends = 1 + (planes - 1) * 5 + 8 * PLANE + 8 * quads + 64
+    n_sends = 1 + (planes - 1) * 16 + 16 * PLANE + 8 * quads + 64
     scratch = {
         "W": vm((quads, 2, rp, dm.wide), BF16),
-        "GU": vm((planes * dm.groups, dm.gs, 2 * dm.ffr), BF16),
+        "GU0": vm((planes * dm.groups, dm.gs, 2 * dm.parts[0][1]), BF16),
+        "GU1": vm((planes * dm.groups, dm.gs, 2 * dm.parts[1][1]), BF16),
         "WD": vm((planes, dm.rfp, dm.d), BF16),
         "nfA": vm((PLANE, tok, dm.d), BF16),
         "gA": vm((PLANE, tok, dm.d), BF16),
@@ -689,7 +763,8 @@
         "dR1": vm((CHIPS, tok, dm.d), BF16),
         "oR2": vm((CHIPS - 1, tok, dm.d), BF16),
         "dR2": vm((CHIPS - 1, tok, dm.d), BF16),
-        "zR": vm((planes + 1, dm.groups, dm.gs, 2 * dm.ffr), BF16),
+        "zR0": vm((planes + 1, dm.groups, dm.gs, 2 * dm.parts[0][1]), BF16),
+        "zR1": vm((planes + 1, dm.groups, dm.gs, 2 * dm.parts[1][1]), BF16),
         "zD": vm((planes + 1, dm.rfp, dm.d), BF16),
         "aR1": vm((quads, rp, dm.wide), BF16),
         "aR2": vm((CHIPS - 1, planes, rp, dm.wide), BF16),
@@ -714,7 +789,8 @@
         "dsem2": sem((CHIPS - 1,)),
         "rA": sem((n,)),
         "rGU": sem((PLANE,)),
-        "rGZ": sem((planes,)),
+        "rGZ0": sem((planes,)),
+        "rGZ1": sem((planes,)),
         "rG": sem((PLANE,)),
         "rWD": sem((planes,)),
         "rNF": sem((PLANE,)),
@@ -722,8 +798,10 @@
         "rD1": sem((CHIPS,)),
         "rO2": sem((CHIPS - 1,)),
         "rD2": sem((CHIPS - 1,)),
-        "rZ": sem((planes + 1,)),
-        "rF": sem((PLANE,)),
+        "rZ0": sem((planes + 1,)),
+        "rZ1": sem((planes + 1,)),
+        "rF0": sem((PLANE,)),
+        "rF1": sem((PLANE,)),
         "rW": sem((planes + 1,)),
         "rA1": sem((planes,)),
         "rA2": sem((CHIPS - 1, planes)),
@@ -782,15 +860,10 @@
 
     both = jnp.stack([columns(w_gate), columns(w_up)], axis=1)
     down = jnp.pad(w_down.reshape(dm.rf, d), ((0, dm.rfp - dm.rf), (0, 0)))
-    half_dim = HEAD_DIM // 2
-    freq = 1000000.0 ** (-(jnp.arange(half_dim).astype(F32) * 2.0 / HEAD_DIM))
-    freq = jnp.tile(freq, LANES // half_dim)[None]
     operands = {
         "x": tokens.reshape(dm.tok, d),
         "g": cotangent.reshape(dm.tok, d),
-        "posc": positions.reshape(dm.tok, 1),
         "posr": positions,
-        "freq": freq,
         "bkey": b_key[None],
         "ap": pack,
         "gus": both,

time: 223 us -> 208 us (0.933)
  Pallas kernels: 195 us -> 180 us
    pallas_call x1, Pallas kernels: 195 us -> 180 us  [run_layer(): pl.pallas_call(functools.partial(layer_kernel, dm, (*operands, *outs, *sc...]
where the time goes in v3:
time: 208 us
  Pallas kernels  180 us (87%)
  local copies, waits for them, and re-layouts  22.9 us (11%)
  other arithmetic  3.39 us (2%)
    pallas_call x1, Pallas kernels, run_layer(): pl.pallas_call(functools.partial(layer_kernel, dm, (*operands, *outs, *sc...  180 us

profile of v3, /device:TPU:0, one launch (start us, length us, event | category | flops | bytes accessed | tf_op | source)
XLA Modules:
  0.0 207.6 jit_solution(3505683707213149432)
XLA Ops:
  0.7 0.8 fusion.11
  1.5 0.9 reshape.98
  2.4 0.9 reshape.101
  3.3 1.4 fusion.8.refs_4_
  5.0 0.7 pad.41.refs_6_
  6.0 1.3 reshape.102
  8.0 0.6 copy-done.6
  8.6 1.3 reshape.103
  10.6 0.9 pad_maximum_fusion.refs_5_
  11.5 180.4 %layer.1 = (bf16[256,896]{1,0:T(8,128)(2,1)}, bf16[256,896]{1,0:T(8,128)(2,1)}, f32[32,2048]{1,0:T(8,128)}, bf16[8,2,32,640]{3,2,1,0:T(8,128)(2,1)}, f32[160,896]{1,0:T(8,128)}) custom-call(bf16[256,896]{1,0:T(8,128)(2,1)} %bitcast.43, bf16[256,896]{1,0:T(8,128)(2,1)} %bitcast.44, s32[2,128]{1,0:T(2,128)} %refs_2_.1, bf16[1,128]{1,0:T(2,128)(2,1)} %bitcast.47, ...), custom_call_target="tpu_custom_call" | custom-call | tf_op jit(solution)/shard_map/layer/pallas_call | solution.py:810
  191.9 1.3 slice_bitcast_fusion.4
  193.1 1.3 slice_bitcast_fusion.3
  194.4 1.4 slice_bitcast_fusion.2
  195.8 1.3 slice_bitcast_fusion
  197.1 1.0 fusion.13
  198.1 0.7 reshape.110
  198.7 0.7 reshape.107
  199.4 0.8 reshape.115
  200.3 0.4 copy-done
  201.9 1.7 reshape.117
  203.9 1.7 reshape.119
  205.6 0.8 copy.37
  206.4 0.4 copy-done.2
  206.8 0.8 copy.38
  (30 shorter events, 3.3 us)
Async XLA Ops:
  0.6 4.0 %copy-start.4 = (bf16[136192]{0:T(1024)(128)(2,1)S(1)}, bf16[136192]{0:T(1024)(128)(2,1)}, u32[]{:S(2)}) copy-start(bf16[136192]{0:T(1024)(128)(2,1)} %param.29) | copy-start | bytes 817156
  5.0 1.0 copy-start.5
  7.7 1.0 copy-start.6
  191.9 7.5 %copy-start.1 = (f32[160,896]{1,0:T(8,128)S(1)}, f32[160,896]{1,0:T(8,128)}, u32[]{:S(2)}) copy-start(f32[160,896]{1,0:T(8,128)} %get-tuple-element.23) | copy-start | bytes 1720324
  199.4 1.3 copy-start
  203.9 1.7 copy-start.3
  205.6 1.2 copy-start.2

commit v4 on v3

--- a/solution.py
+++ b/solution.py
@@ -458,16 +458,27 @@
             device_id_type=MESH,
         )
 
-    def second_copy(k, part, landing, sems, arrive):
-        where = (q + k) % CHIPS
+    diag = CHIPS - 1 - q
+    routes = ((diag, near), (near, near), (next_to, next_to))
+
+    def second_copy(slot, part, landing, sems, arrive):
+        source, to = routes[slot]
         return pltpu.make_async_remote_copy(
-            src_ref=part.at[where, c],
-            dst_ref=landing.at[k - 1],
-            send_sem=sems.at[k - 1],
-            recv_sem=arrive.at[k - 1],
-            device_id=dev(r, where * 2 + c),
+            src_ref=part.at[source, c],
+            dst_ref=landing.at[slot],
+            send_sem=sems.at[slot],
+            recv_sem=arrive.at[slot],
+            device_id=dev(r, to * 2 + c),
             device_id_type=MESH,
         )
+
+    def add_on(part, landing, sems, arrive):
+        arrived(landing.at[0], arrive.at[0])
+        part[next_to, c] = (part[next_to, c].astype(F32) + landing[0].astype(F32)).astype(BF16)
+        second_copy(2, part, landing, sems, arrive).start()
+
+    d_route = (b.dP, b.dR2, b.dsem2, b.rD2)
+    o_route = (b.oP, b.oR2, b.osem2, b.rO2)
 
     def hop(part, landing, arrive, to, cond):
         ahead = (to - r - 1 + planes) // planes
@@ -550,7 +561,9 @@
 
     @pl.loop(0, CHIPS)
     def _(step):
-        where = (q + 1 + step) % CHIPS
+        one, two = (CHIPS - 1 - step) % 2, (CHIPS - 1 - step) // 2
+        over_x, over_y = one * other + two * c, two * other + one * c
+        where = 2 * ((q // 2 + over_y) % 2) + (q % 2 + over_x) % 2
 
         @pl.loop(0, 2)
         def _(turn):
@@ -561,13 +574,17 @@
                 first_copy(where, b.dP, b.dR1, b.dsem, b.rD1).start()
                 first_copy(where, b.oP, b.oR1, b.osem, b.rO1).start()
 
-        @pl.when(step > 0)
-        def _():
-            join((q + step) % CHIPS)
-            second_copy(step, b.dP, b.dR2, b.dsem2, b.rD2).start()
-
-    for k in range(1, CHIPS):
-        second_copy(k, b.oP, b.oR2, b.osem2, b.rO2).start()
+        for at, source in ((1, diag), (2, near)):
+
+            @pl.when(step == at)
+            def _():
+                join(source)
+                second_copy(at - 1, *d_route).start()
+
+    join(next_to)
+    add_on(*d_route)
+    for slot in range(2):
+        second_copy(slot, *o_route).start()
     join(q)
 
     def attn_part(plane):
@@ -580,10 +597,11 @@
     gate_grad(1)
     chain_start(gate_part(1), b.zR1, b.rZ1)
     chain_step(gate_part(0), b.zR0, b.rZ0, 0)
+    add_on(*o_route)
     d_nf = b.dP[q, c].astype(F32)
-    for k in range(1, CHIPS):
-        arrived(b.dR2.at[k - 1], b.rD2.at[k - 1])
-        d_nf = d_nf + b.dR2[k - 1].astype(F32)
+    for slot in (1, 2):
+        arrived(b.dR2.at[slot], b.rD2.at[slot])
+        d_nf = d_nf + b.dR2[slot].astype(F32)
     hidden = b.hid[...]
     scale2 = lax.rsqrt(jnp.mean(hidden * hidden, axis=-1, keepdims=True) + 1e-06)
 
@@ -670,30 +688,30 @@
         arrived(b.aR1.at[quad(to)], b.rA1.at[to])
         mine_now = b.BIG[quad(to), c, :, cols].astype(F32) + b.aR1[quad(to)].astype(F32)
         b.aR1[quad(to)] = mine_now.astype(BF16)
-        for j in range(1, CHIPS):
-            where = (q + j) % CHIPS
-            send(
-                b.aR1.at[to * CHIPS + where],
-                b.aR2.at[j - 1, to],
-                b.rA2.at[j - 1, to],
-                dev(r, where * 2 + c),
-            )
-    total = b.hid[...] + b.oP[q, c].astype(F32)
-    for k in range(1, CHIPS):
-        arrived(b.oR2.at[k - 1], b.rO2.at[k - 1])
-        total = total + b.oR2[k - 1].astype(F32)
-    b.out[...] = total.astype(BF16)
+        for slot in range(2):
+            source, place = routes[slot]
+            send(b.aR1.at[to * CHIPS + source], b.aR2.at[slot, to], b.rA2.at[slot, to], dev(r, place * 2 + c))
     for k in range(1, planes - 1):
         chain_step(gate_part(0), b.zR0, b.rZ0, k)
+    for to in (*far, r):
+        arrived(b.aR2.at[0, to], b.rA2.at[0, to])
+        piece = b.aR1.at[to * CHIPS + next_to]
+        piece[...] = (piece[...].astype(F32) + b.aR2[0, to].astype(F32)).astype(BF16)
+        send(piece, b.aR2.at[2, to], b.rA2.at[2, to], dev(r, next_to * 2 + c))
+    total = b.hid[...] + b.oP[q, c].astype(F32)
+    for slot in (1, 2):
+        arrived(b.oR2.at[slot], b.rO2.at[slot])
+        total = total + b.oR2[slot].astype(F32)
+    b.out[...] = total.astype(BF16)
     for k in range(planes - 1):
         chain_step(down_part, b.zD, b.rW, k)
     for k in range(planes - 2):
         chain_step(gate_part(1), b.zR1, b.rZ1, k)
     for to in (*far, r):
         total = b.aR1[to * CHIPS + q].astype(F32)
-        for j in range(1, CHIPS):
-            arrived(b.aR2.at[j - 1, to], b.rA2.at[j - 1, to])
-            total = total + b.aR2[j - 1, to].astype(F32)
+        for slot in (1, 2):
+            arrived(b.aR2.at[slot, to], b.rA2.at[slot, to])
+            total = total + b.aR2[slot, to].astype(F32)
         b.aR2[0, to] = total.astype(BF16)
     chain_start(attn_part, b.aR3, b.rA3)
     squeeze = b.spr[: dm.unit, : PLANE * rp]
@@ -717,10 +735,25 @@
     home(1, b.zR1, b.rZ1, b.rF1)
     for k in range(planes - 1):
         chain_step(attn_part, b.aR3, b.rA3, k)
-    b.fwd[...] = b.WD[r].astype(F32)
-    chain_end(b.fwd, b.zD, b.rW)
+    sums = b.hid.at[: dm.rfp]
+    sums[...] = b.WD[r].astype(F32)
+    chain_end(sums, b.zD, b.rW)
+
+    def lay_flat(flat, field):
+        blocks = field.shape[1] // LANES
+        for j in range(blocks):
+            flat[pl.ds(j, field.shape[0], stride=blocks), :] = field[:, j * LANES : (j + 1) * LANES]
+
+    lay_flat(b.fd, sums[: dm.rf])
     b.fa[...] = b.aR2[0, r].astype(F32)
     chain_end(b.fa, b.aR3, b.rA3)
+    own_rows = b.fa[: dm.rows]
+    h, kv = dm.heads, dm.kv
+    lay_flat(b.fq, own_rows[:, :h])
+    b.fk[...] = own_rows[:, h : h + kv]
+    b.fv[...] = own_rows[:, h + kv : h + 2 * kv]
+    lay_flat(b.fo, own_rows[:, h + 2 * kv :])
+    b.fs[...] = b.fa[dm.rows : dm.rows + 1, : 2 * LANES]
     for k in range(1, PLANE):
         origin = (p + PLANE - k) % PLANE
         for (start, width), final in zip(dm.parts, (b.rF0, b.rF1)):
@@ -728,9 +761,9 @@
     for where in range(CHIPS):
         first_copy(where, b.oP, b.oR1, b.osem, b.rO1).wait_send()
         first_copy(where, b.dP, b.dR1, b.dsem, b.rD1).wait_send()
-    for k in range(1, CHIPS):
-        second_copy(k, b.oP, b.oR2, b.osem2, b.rO2).wait_send()
-        second_copy(k, b.dP, b.dR2, b.dsem2, b.rD2).wait_send()
+    for slot in range(CHIPS - 1):
+        second_copy(slot, *o_route).wait_send()
+        second_copy(slot, *d_route).wait_send()
     drain()
 
 
@@ -743,9 +776,13 @@
     outs = {
         "out": jax.ShapeDtypeStruct((tok, dm.d), BF16),
         "gin": jax.ShapeDtypeStruct((tok, dm.d), BF16),
-        "fa": jax.ShapeDtypeStruct((rp, dm.wide), F32),
+        "fq": jax.ShapeDtypeStruct((dm.rows * dm.heads // LANES, LANES), F32),
+        "fk": jax.ShapeDtypeStruct((dm.rows, LANES), F32),
+        "fv": jax.ShapeDtypeStruct((dm.rows, LANES), F32),
+        "fo": jax.ShapeDtypeStruct((dm.rows * dm.d // LANES, LANES), F32),
+        "fs": jax.ShapeDtypeStruct((1, 2 * LANES), F32),
         "fgu": jax.ShapeDtypeStruct((PLANE, 2, rp, dm.ffr), BF16),
-        "fwd": jax.ShapeDtypeStruct((dm.rfp, dm.d), F32),
+        "fd": jax.ShapeDtypeStruct((dm.rf * dm.d // LANES, LANES), F32),
     }
     n_sends = 1 + (planes - 1) * 16 + 16 * PLANE + 8 * quads + 64
     scratch = {
@@ -772,6 +809,7 @@
         "QS": vm((dm.micro, HEADS * dm.slots, LANES), BF16),
         "PF": vm((dm.micro, HEADS * dm.slots, dm.slots), F32),
         "hid": vm((tok, dm.d), F32),
+        "fa": vm((rp, dm.wide), F32),
         "dhid": vm((tok, dm.d), F32),
         "npad": vm((tok, dm.dp), BF16),
         "mpad": vm((tok, dm.dp), BF16),
@@ -869,35 +907,31 @@
         "gus": both,
         "wds": down,
     }
-    out, gin, fa, fgu, fwd = run_layer(dm, operands)
+    out, gin, fq, fk, fv, fo, fs, fgu, fd = run_layer(dm, operands)
 
     def field(i, size):
-        return fa[rows, i * FIELD : i * FIELD + size]
-
-    def flat(start, stop):
-        return fa[:rows, start:stop].reshape(-1)
+        return fs[0, i * FIELD : i * FIELD + size]
 
     def gate_part(i):
         part = fgu[:, i, :rows].astype(F32)
         part = part.reshape(PLANE, rows, dm.planes, dm.rfp)[..., : dm.rf]
         return part.transpose(1, 2, 0, 3).reshape(-1)
 
-    h, kv = dm.heads, dm.kv
     return (
         out.reshape(micro, slots, d),
         gin.reshape(micro, slots, d),
         field(0, rows),
-        flat(0, h),
+        fq.reshape(-1),
         field(1, rows),
-        flat(h, h + kv),
-        fa[rows, LANES : LANES + kv],
-        flat(h + kv, h + 2 * kv),
+        fk.reshape(-1),
+        fs[0, LANES : LANES + dm.kv],
+        fv.reshape(-1),
         field(3, dm.rv),
-        flat(h + 2 * kv, dm.wide),
+        fo.reshape(-1),
         field(2, rows),
         gate_part(0),
         gate_part(1),
-        fwd[: dm.rf].reshape(-1),
+        fd.reshape(-1),
     )
 
 

time: 208 us -> 202 us (0.971)
  Pallas kernels: 180 us -> 176 us
    pallas_call x1, Pallas kernels: 180 us -> 176 us  [run_layer(): pl.pallas_call(functools.partial(layer_kernel, dm, (*operands, *outs, *sc...]
    unnamed x16 -> x29, local copies, waits for them, and re-layouts: 3.31 us -> 7.21 us
    reshape x4 -> x0, local copies, waits for them, and re-layouts: 3.49 us -> none  [the longest x3 2.65 us: flat(): return fa[:rows, start:stop].reshape(-1)]
    squeeze x3, local copies, waits for them, and re-layouts: 3.89 us -> 1.68 us  [the longest x2 1.17 us: field(): return fs[0, i * FIELD:i * FIELD + size]]
where the time goes in v4:
time: 202 us; the launch traced here: 201 us
  Pallas kernels  176 us (87%)
  local copies, waits for them, and re-layouts  21.2 us (10%)
  other arithmetic  3.4 us (2%)
    pallas_call x1, Pallas kernels, run_layer(): pl.pallas_call(functools.partial(layer_kernel, dm, (*operands, *outs, *sc...  176 us
    unnamed x29, local copies, waits for them, and re-layouts  7.21 us

profile of v4, /device:TPU:0, one launch (start us, length us, event | category | flops | bytes accessed | tf_op | source)
XLA Modules:
  0.0 201.2 jit_solution(10712013265994227891)
XLA Ops:
  0.7 0.8 fusion.11
  1.5 0.9 reshape.98
  2.4 0.9 reshape.101
  3.3 1.4 fusion.8.refs_4_
  5.0 0.7 pad.41.refs_6_
  6.0 1.3 reshape.102
  8.0 0.6 copy-done.5
  8.6 1.3 reshape.103
  10.6 0.9 pad_maximum_fusion.refs_5_
  11.5 175.7 %layer.1 = (bf16[256,896]{1,0:T(8,128)(2,1)}, bf16[256,896]{1,0:T(8,128)(2,1)}, f32[196,128]{1,0:T(8,128)}, f32[28,128]{1,0:T(8,128)}, f32[28,128]{1,0:T(8,128)}...) custom-call(bf16[256,896]{1,0:T(8,128)(2,1)} %bitcast.45, ...), custom_call_target="tpu_custom_call" | custom-call | tf_op jit(solution)/shard_map/layer/pallas_call | solution.py:848
  187.2 0.6 copy-done.10
  187.8 0.5 slice_bitcast_fusion.2
  188.3 0.6 slice_bitcast_fusion.1
  188.9 0.6 slice_bitcast_fusion
  189.5 1.1 fusion.12
  191.8 1.7 reshape.117
  193.8 1.7 reshape.119
  195.5 0.8 copy.42
  196.7 0.8 copy.43
  197.6 0.6 copy.44
  198.4 0.6 copy.45
  199.1 0.6 copy.46
  199.7 0.6 copy.47
  200.3 0.8 copy.48
  (37 shorter events, 4.0 us)
Async XLA Ops:
  0.6 4.0 %copy-start.3 = (bf16[136192]{0:T(1024)(128)(2,1)S(1)}, bf16[136192]{0:T(1024)(128)(2,1)}, u32[]{:S(2)}) copy-start(bf16[136192]{0:T(1024)(128)(2,1)} %param.29) | copy-start | bytes 817156
  5.0 1.0 copy-start.4
  7.7 1.0 copy-start.5
  187.2 0.6 copy-start.10
  193.8 1.7 copy-start.2
  195.5 1.2 copy-start.1
  196.7 1.0 copy-start.7
  196.7 3.7 %copy-start = (f32[1064,128]{1,0:T(8,128)S(1)}, f32[1064,128]{1,0:T(8,128)}, u32[]{:S(2)}) copy-start(f32[1064,128]{1,0:T(8,128)} %get-tuple-element.31) | copy-start | bytes 1634308
  197.6 0.7 copy-start.9
  197.6 2.0 %copy-start.6 = (f32[196,128]{1,0:T(8,128)S(1)}, f32[196,128]{1,0:T(8,128)}, u32[]{:S(2)}) copy-start(f32[196,128]{1,0:T(8,128)} %get-tuple-element.29) | copy-start | bytes 301060
  198.4 0.7 copy-start.8

commit v5 on v4

--- a/solution.py
+++ b/solution.py
@@ -72,8 +72,8 @@
         self.gs = 16 if self.unit % 16 == 0 else 8
         self.groups = self.unit // self.gs
         blocks = self.ffr // LANES
-        wide = (blocks + 1) // 2 * LANES
-        self.parts = ((0, wide), (wide, self.ffr - wide))
+        first = blocks // 2 * LANES
+        self.parts = ((0, first), (first, self.ffr - first))
 
 
 def spread_matrix(dm):
@@ -251,13 +251,12 @@
             send(src, ref.at[p], arrive.at[p], dev(r, where * 2 + c))
         send(src, ref.at[p], arrive.at[p], (partner,))
 
-    def take_in(ref, arrive):
-        for i, where in enumerate(spots):
-            place = where * 2 + c
-            arrived(ref.at[place], arrive.at[place])
-            if i == 0:
-                send(ref.at[place], ref.at[place], arrive.at[place], dev(r, next_to * 2 + c))
-            send(ref.at[place], ref.at[place], arrive.at[place], (partner,))
+    def hand_on(ref, arrive, where):
+        place = where * 2 + c
+        arrived(ref.at[place], arrive.at[place])
+        if where is near:
+            send(ref.at[place], ref.at[place], arrive.at[place], dev(r, next_to * 2 + c))
+        send(ref.at[place], ref.at[place], arrive.at[place], (partner,))
 
     fan(me, b.ap)
     send(b.ap, block(b.W, me), b.rA.at[me], (partner,))
@@ -404,11 +403,15 @@
 
     spread_out(b.nfA.at[p], b.nfA, b.rNF)
     pass_on(*gate_on[0][0])
-    relay_own(gate_part(1)(r), gate_part(1)(r), b.rGZ1.at[r], "gate1")
-    take_in(b.gA, b.rG)
+    hand_on(b.gA, b.rG, near)
     for item in gate_on[0][1:]:
         pass_on(*item)
-    take_in(b.nfA, b.rNF)
+    relay_own(gate_part(1)(r), gate_part(1)(r), b.rGZ1.at[r], "gate1")
+    hand_on(b.nfA, b.rNF, near)
+    for where in spots[1:]:
+        hand_on(b.gA, b.rG, where)
+    for where in spots[1:]:
+        hand_on(b.nfA, b.rNF, where)
     for item in (*down_on, *gate_on[0]):
         settle(*item)
     pass_on(*gate_on[1][0])
@@ -596,7 +599,8 @@
     drain("gate1")
     gate_grad(1)
     chain_start(gate_part(1), b.zR1, b.rZ1)
-    chain_step(gate_part(0), b.zR0, b.rZ0, 0)
+    for k in range(planes - 1):
+        chain_step(gate_part(0), b.zR0, b.rZ0, k)
     add_on(*o_route)
     d_nf = b.dP[q, c].astype(F32)
     for slot in (1, 2):
@@ -617,6 +621,7 @@
     d_hidden = b.g[...].astype(F32) + d_part
     b.dhid[...] = d_hidden
     d_attn = d_hidden.astype(BF16)
+    chain_step(down_part, b.zD, b.rW, 0)
     BIG[:, dm.qkv : dm.wide] = mm_tn(b.mpad[...], d_attn).astype(BF16)
     d_mixed = mm_nt(d_attn, W[:, dm.qkv :]).astype(BF16)
     d_mixed = mm_nt(d_mixed, b.spr[...])
@@ -688,25 +693,24 @@
         arrived(b.aR1.at[quad(to)], b.rA1.at[to])
         mine_now = b.BIG[quad(to), c, :, cols].astype(F32) + b.aR1[quad(to)].astype(F32)
         b.aR1[quad(to)] = mine_now.astype(BF16)
-        for slot in range(2):
-            source, place = routes[slot]
-            send(b.aR1.at[to * CHIPS + source], b.aR2.at[slot, to], b.rA2.at[slot, to], dev(r, place * 2 + c))
+        send(b.aR1.at[to * CHIPS + diag], b.aR2.at[0, to], b.rA2.at[0, to], dev(r, near * 2 + c))
+    for to in (*far, r):
+        send(b.aR1.at[to * CHIPS + near], b.aR2.at[1, to], b.rA2.at[1, to], dev(r, near * 2 + c))
     for k in range(1, planes - 1):
-        chain_step(gate_part(0), b.zR0, b.rZ0, k)
+        chain_step(down_part, b.zD, b.rW, k)
+    chain_step(gate_part(1), b.zR1, b.rZ1, 0)
     for to in (*far, r):
         arrived(b.aR2.at[0, to], b.rA2.at[0, to])
         piece = b.aR1.at[to * CHIPS + next_to]
         piece[...] = (piece[...].astype(F32) + b.aR2[0, to].astype(F32)).astype(BF16)
         send(piece, b.aR2.at[2, to], b.rA2.at[2, to], dev(r, next_to * 2 + c))
+    for k in range(1, planes - 2):
+        chain_step(gate_part(1), b.zR1, b.rZ1, k)
     total = b.hid[...] + b.oP[q, c].astype(F32)
     for slot in (1, 2):
         arrived(b.oR2.at[slot], b.rO2.at[slot])
         total = total + b.oR2[slot].astype(F32)
     b.out[...] = total.astype(BF16)
-    for k in range(planes - 1):
-        chain_step(down_part, b.zD, b.rW, k)
-    for k in range(planes - 2):
-        chain_step(gate_part(1), b.zR1, b.rZ1, k)
     for to in (*far, r):
         total = b.aR1[to * CHIPS + q].astype(F32)
         for slot in (1, 2):

time: 202 us -> 192 us (0.950)
  Pallas kernels: 176 us -> 166 us
    pallas_call x1, Pallas kernels: 176 us -> 166 us  [run_layer(): pl.pallas_call(functools.partial(layer_kernel, dm, (*operands, *outs, *sc...]
where the time goes in v5:
time: 192 us
  Pallas kernels  166 us (86%)
  local copies, waits for them, and re-layouts  21.2 us (11%)
  other arithmetic  3.4 us (2%)
    pallas_call x1, Pallas kernels, run_layer(): pl.pallas_call(functools.partial(layer_kernel, dm, (*operands, *outs, *sc...  166 us
    unnamed x29, local copies, waits for them, and re-layouts  7.21 us

profile of v5, /device:TPU:0, one launch (start us, length us, event | category | flops | bytes accessed | tf_op | source)
XLA Modules:
  0.0 191.5 jit_solution(68213324999143789)
XLA Ops:
  0.7 0.8 fusion.11
  1.5 0.9 reshape.98
  2.4 0.9 reshape.101
  3.3 1.4 fusion.8.refs_4_
  5.0 0.7 pad.41.refs_6_
  6.0 1.3 reshape.102
  8.0 0.6 copy-done.5
  8.6 1.3 reshape.103
  10.6 0.9 pad_maximum_fusion.refs_5_
  11.5 166.1 %layer.1 = (bf16[256,896]{1,0:T(8,128)(2,1)}, bf16[256,896]{1,0:T(8,128)(2,1)}, f32[196,128]{1,0:T(8,128)}, f32[28,128]{1,0:T(8,128)}, f32[28,128]{1,0:T(8,128)}...) custom-call(bf16[256,896]{1,0:T(8,128)(2,1)} %bitcast.45, ...), custom_call_target="tpu_custom_call" | custom-call | tf_op jit(solution)/shard_map/layer/pallas_call | solution.py:852
  177.6 0.6 copy-done.10
  178.2 0.5 slice_bitcast_fusion.2
  178.7 0.6 slice_bitcast_fusion.1
  179.3 0.6 slice_bitcast_fusion
  179.9 1.1 fusion.12
  182.1 1.7 reshape.117
  184.2 1.7 reshape.119
  185.8 0.8 copy.42
  187.0 0.8 copy.43
  188.0 0.6 copy.44
  188.7 0.6 copy.45
  189.4 0.6 copy.46
  190.0 0.6 copy.47
  190.7 0.8 copy.48
  (37 shorter events, 4.0 us)
Async XLA Ops:
  0.6 4.0 %copy-start.3 = (bf16[136192]{0:T(1024)(128)(2,1)S(1)}, bf16[136192]{0:T(1024)(128)(2,1)}, u32[]{:S(2)}) copy-start(bf16[136192]{0:T(1024)(128)(2,1)} %param.29) | copy-start | bytes 817156
  5.0 1.0 copy-start.4
  7.7 1.0 copy-start.5
  177.6 0.6 copy-start.10
  184.1 1.7 copy-start.2
  185.8 1.2 copy-start.1
  187.0 1.0 copy-start.7
  187.0 3.7 %copy-start = (f32[1064,128]{1,0:T(8,128)S(1)}, f32[1064,128]{1,0:T(8,128)}, u32[]{:S(2)}) copy-start(f32[1064,128]{1,0:T(8,128)} %get-tuple-element.31) | copy-start | bytes 1634308
  188.0 0.7 copy-start.9
  188.0 2.0 %copy-start.6 = (f32[196,128]{1,0:T(8,128)S(1)}, f32[196,128]{1,0:T(8,128)}, u32[]{:S(2)}) copy-start(f32[196,128]{1,0:T(8,128)} %get-tuple-element.29) | copy-start | bytes 301060
  188.7 0.7 copy-start.8

commit v6 on v5

--- a/solution.py
+++ b/solution.py
@@ -408,13 +408,15 @@
         pass_on(*item)
     relay_own(gate_part(1)(r), gate_part(1)(r), b.rGZ1.at[r], "gate1")
     hand_on(b.nfA, b.rNF, near)
+    pass_on(*gate_on[1][0])
     for where in spots[1:]:
         hand_on(b.gA, b.rG, where)
     for where in spots[1:]:
         hand_on(b.nfA, b.rNF, where)
+    for item in gate_on[1][1:]:
+        pass_on(*item)
     for item in (*down_on, *gate_on[0]):
         settle(*item)
-    pass_on(*gate_on[1][0])
     keep[2].wait()
     keep[3].wait()
     for k in range(CHIPS):
@@ -545,11 +547,6 @@
     @pl.loop(0, PLANE)
     def _(turn):
         feed(0, turn // 2, turn % 2)
-
-        @pl.when(turn == half - 1)
-        def _():
-            for item in gate_on[1][1:]:
-                pass_on(*item)
 
     drain("gate0")
     gate_grad(0)

time: 192 us -> 187 us (0.974)
  Pallas kernels: 166 us -> 161 us
    pallas_call x1, Pallas kernels: 166 us -> 161 us  [run_layer(): pl.pallas_call(functools.partial(layer_kernel, dm, (*operands, *outs, *sc...]
where the time goes in v6:
time: 187 us; the launch traced here: 186 us
  Pallas kernels  161 us (86%)
  local copies, waits for them, and re-layouts  21.2 us (11%)
  other arithmetic  3.4 us (2%)
    pallas_call x1, Pallas kernels, run_layer(): pl.pallas_call(functools.partial(layer_kernel, dm, (*operands, *outs, *sc...  161 us
    unnamed x29, local copies, waits for them, and re-layouts  7.21 us

profile of v6, /device:TPU:0, one launch (start us, length us, event | category | flops | bytes accessed | tf_op | source)
XLA Modules:
  0.0 186.1 jit_solution(2393727699399381173)
XLA Ops:
  0.7 0.8 fusion.11
  1.5 0.9 reshape.98
  2.4 0.9 reshape.101
  3.3 1.4 fusion.8.refs_4_
  5.0 0.7 pad.41.refs_6_
  6.0 1.3 reshape.102
  8.0 0.6 copy-done.5
  8.6 1.3 reshape.103
  10.6 0.9 pad_maximum_fusion.refs_5_
  11.5 160.7 %layer.1 = (bf16[256,896]{1,0:T(8,128)(2,1)}, bf16[256,896]{1,0:T(8,128)(2,1)}, f32[196,128]{1,0:T(8,128)}, f32[28,128]{1,0:T(8,128)}, f32[28,128]{1,0:T(8,128)}...) custom-call(bf16[256,896]{1,0:T(8,128)(2,1)} %bitcast.45, ...), custom_call_target="tpu_custom_call" | custom-call | tf_op jit(solution)/shard_map/layer/pallas_call | solution.py:849
  172.2 0.6 copy-done.10
  172.8 0.5 slice_bitcast_fusion.2
  173.3 0.6 slice_bitcast_fusion.1
  173.9 0.6 slice_bitcast_fusion
  174.5 1.1 fusion.12
  176.8 1.7 reshape.117
  178.8 1.7 reshape.119
  180.4 0.8 copy.42
  181.6 0.8 copy.43
  182.6 0.6 copy.44
  183.3 0.6 copy.45
  184.0 0.6 copy.46
  184.7 0.6 copy.47
  185.3 0.8 copy.48
  (37 shorter events, 4.0 us)
Async XLA Ops:
  0.6 4.0 %copy-start.3 = (bf16[136192]{0:T(1024)(128)(2,1)S(1)}, bf16[136192]{0:T(1024)(128)(2,1)}, u32[]{:S(2)}) copy-start(bf16[136192]{0:T(1024)(128)(2,1)} %param.29) | copy-start | bytes 817156
  5.0 1.0 copy-start.4
  7.7 1.0 copy-start.5
  172.2 0.6 copy-start.10
  178.7 1.7 copy-start.2
  180.4 1.2 copy-start.1
  181.6 1.0 copy-start.7
  181.6 3.7 %copy-start = (f32[1064,128]{1,0:T(8,128)S(1)}, f32[1064,128]{1,0:T(8,128)}, u32[]{:S(2)}) copy-start(f32[1064,128]{1,0:T(8,128)} %get-tuple-element.31) | copy-start | bytes 1634308
  182.6 0.7 copy-start.9
  182.6 2.0 %copy-start.6 = (f32[196,128]{1,0:T(8,128)S(1)}, f32[196,128]{1,0:T(8,128)}, u32[]{:S(2)}) copy-start(f32[196,128]{1,0:T(8,128)} %get-tuple-element.29) | copy-start | bytes 301060
  183.3 0.7 copy-start.8

commit v7 on v6

--- a/solution.py
+++ b/solution.py
@@ -746,6 +746,35 @@
             flat[pl.ds(j, field.shape[0], stride=blocks), :] = field[:, j * LANES : (j + 1) * LANES]
 
     lay_flat(b.fd, sums[: dm.rf])
+    for k in range(1, PLANE):
+        origin = (p + PLANE - k) % PLANE
+        for (start, width), final in zip(dm.parts, (b.rF0, b.rF1)):
+            arrived(b.fgu.at[origin, :, :, pl.ds(start, width)], final.at[origin])
+    blocks = dm.ff // LANES
+
+    def window(i, run, start):
+        plane, place = run // PLANE, run % PLANE
+        at = plane * dm.rfp + start
+        low = at // LANES * LANES
+        top = min(low + 2 * LANES, dm.ffr)
+        field = b.fgu[place, i, :, low:top].astype(F32)
+        if at > low:
+            field = pltpu.roll(field, top - at, 1)
+        return field[:, :LANES]
+
+    lane = iota((rp, LANES), 1)
+    for i, flat in enumerate((b.fg, b.fu)):
+        for j in range(blocks):
+            run, start = (j * LANES) // dm.rf, (j * LANES) % dm.rf
+            field = window(i, run, start)
+            left = dm.rf - start
+            while left < LANES:
+                run += 1
+                nxt = window(i, run, 0)
+                field = jnp.where(lane < left, field, pltpu.roll(nxt, left, 1))
+                left += dm.rf
+            flat[pl.ds(j, dm.rows, stride=blocks), :] = field[: dm.rows]
+
     b.fa[...] = b.aR2[0, r].astype(F32)
     chain_end(b.fa, b.aR3, b.rA3)
     own_rows = b.fa[: dm.rows]
@@ -755,10 +784,6 @@
     b.fv[...] = own_rows[:, h + kv : h + 2 * kv]
     lay_flat(b.fo, own_rows[:, h + 2 * kv :])
     b.fs[...] = b.fa[dm.rows : dm.rows + 1, : 2 * LANES]
-    for k in range(1, PLANE):
-        origin = (p + PLANE - k) % PLANE
-        for (start, width), final in zip(dm.parts, (b.rF0, b.rF1)):
-            arrived(b.fgu.at[origin, :, :, pl.ds(start, width)], final.at[origin])
     for where in range(CHIPS):
         first_copy(where, b.oP, b.oR1, b.osem, b.rO1).wait_send()
         first_copy(where, b.dP, b.dR1, b.dsem, b.rD1).wait_send()
@@ -782,7 +807,8 @@
         "fv": jax.ShapeDtypeStruct((dm.rows, LANES), F32),
         "fo": jax.ShapeDtypeStruct((dm.rows * dm.d // LANES, LANES), F32),
         "fs": jax.ShapeDtypeStruct((1, 2 * LANES), F32),
-        "fgu": jax.ShapeDtypeStruct((PLANE, 2, rp, dm.ffr), BF16),
+        "fg": jax.ShapeDtypeStruct((dm.rows * dm.ff // LANES, LANES), F32),
+        "fu": jax.ShapeDtypeStruct((dm.rows * dm.ff // LANES, LANES), F32),
         "fd": jax.ShapeDtypeStruct((dm.rf * dm.d // LANES, LANES), F32),
     }
     n_sends = 1 + (planes - 1) * 16 + 16 * PLANE + 8 * quads + 64
@@ -811,6 +837,7 @@
         "PF": vm((dm.micro, HEADS * dm.slots, dm.slots), F32),
         "hid": vm((tok, dm.d), F32),
         "fa": vm((rp, dm.wide), F32),
+        "fgu": vm((PLANE, 2, rp, dm.ffr), BF16),
         "dhid": vm((tok, dm.d), F32),
         "npad": vm((tok, dm.dp), BF16),
         "mpad": vm((tok, dm.dp), BF16),
@@ -908,15 +935,10 @@
         "gus": both,
         "wds": down,
     }
-    out, gin, fq, fk, fv, fo, fs, fgu, fd = run_layer(dm, operands)
+    out, gin, fq, fk, fv, fo, fs, fg, fu, fd = run_layer(dm, operands)
 
     def field(i, size):
         return fs[0, i * FIELD : i * FIELD + size]
-
-    def gate_part(i):
-        part = fgu[:, i, :rows].astype(F32)
-        part = part.reshape(PLANE, rows, dm.planes, dm.rfp)[..., : dm.rf]
-        return part.transpose(1, 2, 0, 3).reshape(-1)
 
     return (
         out.reshape(micro, slots, d),
@@ -930,8 +952,8 @@
         field(3, dm.rv),
         fo.reshape(-1),
         field(2, rows),
-        gate_part(0),
-        gate_part(1),
+        fg.reshape(-1),
+        fu.reshape(-1),
         fd.reshape(-1),
     )
 

time: 187 us -> 185 us (0.989)
  local copies, waits for them, and re-layouts: 21.2 us -> 18.8 us
    reshape x4 -> x0, local copies, waits for them, and re-layouts: 3.71 us -> none  [gate_part(): return part.transpose(1, 2, 0, 3).reshape(-1)]
    unnamed x29 -> x33, local copies, waits for them, and re-layouts: 7.21 us -> 10.4 us
where the time goes in v7:
time: 185 us; the launch traced here: 183 us
  Pallas kernels  161 us (87%)
  local copies, waits for them, and re-layouts  18.8 us (10%)
  other arithmetic  3.15 us (2%)
    pallas_call x1, Pallas kernels, run_layer(): pl.pallas_call(functools.partial(layer_kernel, dm, (*operands, *outs, *sc...  161 us
    unnamed x33, local copies, waits for them, and re-layouts  10.4 us

profile of v7, /device:TPU:0, one launch (start us, length us, event | category | flops | bytes accessed | tf_op | source)
XLA Modules:
  0.0 183.4 jit_solution(10227608524455039320)
XLA Ops:
  0.7 0.8 fusion.11
  1.5 0.9 reshape.84
  2.4 0.9 reshape.87
  3.3 1.4 fusion.8.refs_4_
  5.0 0.7 pad.41.refs_6_
  6.0 1.3 reshape.88
  8.0 0.6 copy-done.6
  8.6 1.3 reshape.89
  10.6 0.9 pad_maximum_fusion.refs_5_
  11.5 160.7 %layer.1 = (bf16[256,896]{1,0:T(8,128)(2,1)}, bf16[256,896]{1,0:T(8,128)(2,1)}, f32[196,128]{1,0:T(8,128)}, f32[28,128]{1,0:T(8,128)}, f32[28,128]{1,0:T(8,128)}...) custom-call(bf16[256,896]{1,0:T(8,128)(2,1)} %bitcast.33, ...), custom_call_target="tpu_custom_call" | custom-call | tf_op jit(solution)/shard_map/layer/pallas_call | solution.py:876
  172.2 0.7 copy-done.11
  172.9 0.5 slice_bitcast_fusion.2
  173.4 0.6 slice_bitcast_fusion.1
  174.0 0.6 slice_bitcast_fusion
  174.6 1.9 %copy.40 = bf16[2,128,896]{2,1,0:T(8,128)(2,1)} copy(bf16[2,128,896]{2,1,0:T(8,128)(2,1)} %bitcast.32) | data formatting | bytes 917504
  176.4 0.8 copy.41
  177.4 0.6 copy.42
  178.1 0.6 copy.43
  178.8 0.6 copy.44
  179.5 0.6 copy.45
  180.1 0.8 copy.46
  181.4 0.8 copy.47
  182.2 0.4 copy-done
  182.6 0.8 copy.48
  (30 shorter events, 2.6 us)
Async XLA Ops:
  0.6 4.0 %copy-start.4 = (bf16[136192]{0:T(1024)(128)(2,1)S(1)}, bf16[136192]{0:T(1024)(128)(2,1)}, u32[]{:S(2)}) copy-start(bf16[136192]{0:T(1024)(128)(2,1)} %param.29) | copy-start | bytes 817156
  5.0 1.0 copy-start.5
  7.6 1.0 copy-start.6
  172.2 0.7 copy-start.11
  174.6 1.9 %copy-start.3 = (bf16[256,896]{1,0:T(8,128)(2,1)S(1)}, bf16[256,896]{1,0:T(8,128)(2,1)}, u32[]{:S(2)}) copy-start(bf16[256,896]{1,0:T(8,128)(2,1)} %get-tuple-element.25) | copy-start | bytes 1376260
  176.4 1.0 copy-start.8
  176.4 3.7 %copy-start.2 = (f32[1064,128]{1,0:T(8,128)S(1)}, f32[1064,128]{1,0:T(8,128)}, u32[]{:S(2)}) copy-start(f32[1064,128]{1,0:T(8,128)} %get-tuple-element.31) | copy-start | bytes 1634308
  177.4 0.7 copy-start.10
  177.4 2.0 %copy-start.7 = (f32[196,128]{1,0:T(8,128)S(1)}, f32[196,128]{1,0:T(8,128)}, u32[]{:S(2)}) copy-start(f32[196,128]{1,0:T(8,128)} %get-tuple-element.30) | copy-start | bytes 301060
  178.1 0.7 copy-start.9
  180.1 1.2 copy-start.1
  181.4 1.2 copy-start

commit v8 on v7

--- a/solution.py
+++ b/solution.py
@@ -228,12 +228,12 @@
 
     keep = [
         pltpu.make_async_copy(b.ap, block(b.W, me), b.csem.at[0]),
-        pltpu.make_async_copy(b.gus.at[p], b.fgu.at[p], b.csem.at[1]),
+        pltpu.make_async_copy(b.act.at[pl.ds(2 * p, 2)], b.fgu.at[p], b.csem.at[1]),
         pltpu.make_async_copy(b.g, b.gA.at[p], b.csem.at[2]),
         pltpu.make_async_copy(b.wds, b.WD.at[r], b.csem.at[3]),
     ]
-    for copy in keep:
-        copy.start()
+    for i in (0, 2, 3):
+        keep[i].start()
 
     relay_own(b.ap, block(b.W, me), b.rA.at[me])
 
@@ -260,9 +260,39 @@
 
     fan(me, b.ap)
     send(b.ap, block(b.W, me), b.rA.at[me], (partner,))
+    relay_own(b.wds, b.WD.at[r], b.rWD.at[r])
+
+    lane = iota((dm.rows, LANES), 1)
+
+    def shifted(read, at, width):
+        low = at // LANES * LANES
+        top = min(low + 2 * LANES, width)
+        field = read(low, top).astype(F32)
+        if at > low:
+            field = pltpu.roll(field, top - at, 1)
+        return field[:, :LANES]
+
+    b.act[: 2 * PLANE] = jnp.zeros((2 * PLANE, rp, dm.ffr), BF16)
+    for i, ref in enumerate((b.wg, b.wu)):
+        for place in range(PLANE):
+            for column in range(0, dm.ffr, LANES):
+                plane, start = column // dm.rfp, column % dm.rfp
+                filled, field = 0, jnp.zeros((dm.rows, LANES), F32)
+                while filled < LANES:
+                    real = dm.rf - start
+                    if real > 0:
+                        at = (plane * PLANE + place) * dm.rf + start
+                        piece = shifted(lambda low, top: ref[:, low:top], at, dm.ff)
+                        if filled:
+                            piece = pltpu.roll(piece, filled, 1)
+                        field = jnp.where((lane >= filled) & (lane < filled + real), piece, field)
+                    filled += dm.rfp - start
+                    plane, start = plane + 1, 0
+                b.act[2 * place + i, : dm.rows, column : column + LANES] = field.astype(BF16)
+    keep[1].start()
     for k in range(1, PLANE):
-        send(b.gus.at[(p + k) % PLANE], b.fgu.at[p], b.rGU.at[p], dev(r, (p + k) % PLANE))
-    relay_own(b.wds, b.WD.at[r], b.rWD.at[r])
+        to = (p + k) % PLANE
+        send(b.act.at[pl.ds(2 * to, 2)], b.fgu.at[p], b.rGU.at[p], dev(r, to), tag="own")
 
     tok = dm.tok
     xf = b.x[...].astype(F32)
@@ -544,6 +574,7 @@
         if dm.d % chunk:
             some(dm.d - dm.d % chunk, dm.d % chunk)
 
+    drain("own")
     @pl.loop(0, PLANE)
     def _(turn):
         feed(0, turn // 2, turn % 2)
@@ -574,12 +605,12 @@
                 first_copy(where, b.dP, b.dR1, b.dsem, b.rD1).start()
                 first_copy(where, b.oP, b.oR1, b.osem, b.rO1).start()
 
-        for at, source in ((1, diag), (2, near)):
-
-            @pl.when(step == at)
-            def _():
-                join(source)
-                second_copy(at - 1, *d_route).start()
+            for at, late, source in ((1, 0, diag), (2, 1, near)):
+
+                @pl.when((step == at) & (turn == late))
+                def _():
+                    join(source)
+                    second_copy(at - 1, *d_route).start()
 
     join(next_to)
     add_on(*d_route)
@@ -753,14 +784,8 @@
     blocks = dm.ff // LANES
 
     def window(i, run, start):
-        plane, place = run // PLANE, run % PLANE
-        at = plane * dm.rfp + start
-        low = at // LANES * LANES
-        top = min(low + 2 * LANES, dm.ffr)
-        field = b.fgu[place, i, :, low:top].astype(F32)
-        if at > low:
-            field = pltpu.roll(field, top - at, 1)
-        return field[:, :LANES]
+        place = run % PLANE
+        return shifted(lambda low, top: b.fgu[place, i, :, low:top], run // PLANE * dm.rfp + start, dm.ffr)
 
     lane = iota((rp, LANES), 1)
     for i, flat in enumerate((b.fg, b.fu)):
@@ -919,12 +944,6 @@
     pack = jnp.concatenate([pack, spare[None]], axis=0)
     pack = jnp.pad(pack, ((0, rp - rows - 1), (0, 0)))
 
-    def columns(weight):
-        weight = weight.reshape(rows, dm.planes, PLANE, dm.rf)
-        weight = jnp.pad(weight, ((0, rp - rows), (0, 0), (0, 0), (0, dm.rfp - dm.rf)))
-        return weight.transpose(2, 0, 1, 3).reshape(PLANE, rp, dm.ffr)
-
-    both = jnp.stack([columns(w_gate), columns(w_up)], axis=1)
     down = jnp.pad(w_down.reshape(dm.rf, d), ((0, dm.rfp - dm.rf), (0, 0)))
     operands = {
         "x": tokens.reshape(dm.tok, d),
@@ -932,7 +951,8 @@
         "posr": positions,
         "bkey": b_key[None],
         "ap": pack,
-        "gus": both,
+        "wg": w_gate.reshape(rows, dm.ff),
+        "wu": w_up.reshape(rows, dm.ff),
         "wds": down,
     }
     out, gin, fq, fk, fv, fo, fs, fg, fu, fd = run_layer(dm, operands)

time: 185 us -> 181 us (0.978)
  local copies, waits for them, and re-layouts: 18.8 us -> 16.4 us
where the time goes in v8:
time: 181 us; the launch traced here: 180 us
  Pallas kernels  161 us (89%)
  local copies, waits for them, and re-layouts  16.4 us (9%)
  other arithmetic  2.23 us (1%)
    pallas_call x1, Pallas kernels, run_layer(): pl.pallas_call(functools.partial(layer_kernel, dm, (*operands, *outs, *sc...  161 us
    unnamed x33, local copies, waits for them, and re-layouts  9.79 us

profile of v8, /device:TPU:0, one launch (start us, length us, event | category | flops | bytes accessed | tf_op | source)
XLA Modules:
  0.0 180.1 jit_solution(8435955138392123687)
XLA Ops:
  0.7 0.8 fusion.11
  1.5 0.9 reshape.84
  2.4 0.9 reshape.87
  3.3 1.4 fusion.8.refs_4_
  4.7 0.3 reshape.90
  5.0 0.7 pad.32.refs_7_
  6.0 1.0 reshape.88.refs_5_
  7.0 1.0 reshape.89.refs_6_
  8.1 160.8 %layer.1 = (bf16[256,896]{1,0:T(8,128)(2,1)}, bf16[256,896]{1,0:T(8,128)(2,1)}, f32[196,128]{1,0:T(8,128)}, f32[28,128]{1,0:T(8,128)}, f32[28,128]{1,0:T(8,128)}...) custom-call(bf16[256,896]{1,0:T(8,128)(2,1)} %bitcast.29, ...), custom_call_target="tpu_custom_call" | custom-call | tf_op jit(solution)/shard_map/layer/pallas_call | solution.py:901
  168.9 0.6 copy-done.11
  169.5 0.5 slice_bitcast_fusion.2
  170.0 0.6 slice_bitcast_fusion.1
  170.6 0.6 slice_bitcast_fusion
  171.2 1.9 %copy.38 = bf16[2,128,896]{2,1,0:T(8,128)(2,1)} copy(bf16[2,128,896]{2,1,0:T(8,128)(2,1)} %bitcast.28) | data formatting | bytes 917504
  173.1 0.8 copy.39
  174.1 0.6 copy.40
  174.8 0.6 copy.41
  175.5 0.6 copy.42
  176.1 0.6 copy.43
  176.8 0.8 copy.44
  177.6 0.4 copy-done.1
  178.0 0.8 copy.45
  178.9 0.4 copy-done
  179.3 0.8 copy.46
  (23 shorter events, 0.7 us)
Async XLA Ops:
  0.6 4.0 %copy-start.4 = (bf16[136192]{0:T(1024)(128)(2,1)S(1)}, bf16[136192]{0:T(1024)(128)(2,1)}, u32[]{:S(2)}) copy-start(bf16[136192]{0:T(1024)(128)(2,1)} %param.29) | copy-start | bytes 817156
  5.0 1.0 copy-start.5
  6.0 1.0 copy-start.6
  168.9 0.6 copy-start.11
  171.2 1.9 %copy-start.3 = (bf16[256,896]{1,0:T(8,128)(2,1)S(1)}, bf16[256,896]{1,0:T(8,128)(2,1)}, u32[]{:S(2)}) copy-start(bf16[256,896]{1,0:T(8,128)(2,1)} %get-tuple-element.25) | copy-start | bytes 1376260
  173.1 1.0 copy-start.8
  173.1 3.7 %copy-start.2 = (f32[1064,128]{1,0:T(8,128)S(1)}, f32[1064,128]{1,0:T(8,128)}, u32[]{:S(2)}) copy-start(f32[1064,128]{1,0:T(8,128)} %get-tuple-element.31) | copy-start | bytes 1634308
  174.1 0.7 copy-start.10
  174.1 2.0 %copy-start.7 = (f32[196,128]{1,0:T(8,128)S(1)}, f32[196,128]{1,0:T(8,128)}, u32[]{:S(2)}) copy-start(f32[196,128]{1,0:T(8,128)} %get-tuple-element.30) | copy-start | bytes 301060
  174.8 0.7 copy-start.9
  176.8 1.2 copy-start.1
  178.0 1.2 copy-start
